TPU v7x, 32 devices: a whole 2x2x4 slice. The times are simulated.
32 devices in a mesh: slab: 2 (over y), tp: 4 (over x, core), band: 4 (over z).
Axes of the slice: x: 2, y: 2, z: 4, core: 2. Of those that a mesh axis runs over, the one named last changes fastest.
Arguments:
- tokens: bfloat16 [3072, 3072], P(('slab', 'band'), 'tp'), may hold values from -6 to 6
- w_qkv: bfloat16 [3072, 3, 3072], P('band', None, 'tp'), may hold values from -0.109375 to 0.109375
- w_out: bfloat16 [3072, 3072], P('tp'), may hold values from -0.109375 to 0.109375
- shift: float32 [3072], replicated, may hold values from -3 to 3
- scale: float32 [3072], replicated, may hold values from -0.9 to 0.9
- gate: float32 [3072], P('tp'), may hold values from 0.5 to 2
- q_gain: float32 [128], replicated, may hold values from 0.5 to 5.5
- k_gain: float32 [128], replicated, may hold values from 0.5 to 5.5
- tile_ids: int32 [24, 14], P(('slab', 'band')), may hold values from 0 to 23, as said below
- key_counts: int32 [24], P(('slab', 'band')), may hold values from 1 to 14, as said below
Outputs:
- update: bfloat16 [3072, 3072], P(('slab', 'band'), 'tp')
Inputs may be any that keep to these rules, and one draw needn't show every extreme that they name: `tile_ids`: row q's first key_counts[q] entries are distinct tiles, the first being q itself, whose time index (tile // 12), row index ((tile // 3) % 4) and column index (tile % 3) each differ from q's by at most one; the remaining entries equal q. `key_counts`: 14 is reached in every draw.
All inputs are finite; a program needn't handle non-finite values.
Results may differ from a plain program's by a relative error of at most 0.014.
The roundings to bfloat16 on the way count: a program that leaves them out, or rounds other values in their place, can miss the bound.
Values may be sent and summed in bfloat16 or wider, within the bound.
A program may use at most 128 MiB of HBM per device.

v0:
```python
import jax
import jax.numpy as jnp
from jax import lax
from jax.sharding import PartitionSpec as P


def padded_2(block, sides, width):
    for axis, dim in sides:
        count = lax.axis_size(axis)
        forward = [(i, i + 1) for i in range(count - 1)]
        backward = [(target, source) for source, target in forward]
        low = lax.ppermute(
            lax.slice_in_dim(block, block.shape[dim] - width, None, axis=dim), axis, forward
        )
        high = lax.ppermute(lax.slice_in_dim(block, 0, width, axis=dim), axis, backward)
        block = jnp.concatenate([low, block, high], axis=dim)
    return block


def head_norm(part, gain):
    squares = jnp.mean(part * part, axis=-1, keepdims=True)
    return (part * lax.rsqrt(squares + 1e-06) * gain).astype(jnp.bfloat16)


def attend(query, near, allowed, head_feats, head_size):
    many = near.shape[0]
    tile_len = near.shape[1]
    heads = head_feats // head_size
    near_keys = near[:, :, :head_feats].reshape(many * tile_len, heads, head_size)
    near_values = near[:, :, head_feats:].reshape(many * tile_len, heads, head_size)
    scores = jnp.einsum("qhd,khd->hqk", query, near_keys, preferred_element_type=jnp.float32)
    scores = scores * (1.0 / head_size**0.5)
    token_mask = jnp.repeat(allowed, tile_len)
    scores = jnp.where(token_mask[None, None, :], scores, -1e30)
    top = jnp.max(scores, axis=-1, keepdims=True)
    weights = jnp.exp(scores - top)
    probs = (weights / jnp.sum(weights, axis=-1, keepdims=True)).astype(jnp.bfloat16)
    result = jnp.einsum("hqk,khd->qhd", probs, near_values, preferred_element_type=jnp.float32)
    return result.astype(jnp.bfloat16).reshape(tile_len, head_feats)


def shards(tokens, w_qkv, w_out, shift, scale, gate, q_gain, k_gain, tile_ids, key_counts):
    whole = lax.all_gather(tokens, "tp", axis=1, tiled=True)
    tok_rows = whole.shape[0]
    head_feats = w_out.shape[0]
    head_size = q_gain.shape[0]
    heads = head_feats // head_size
    tiles = key_counts.shape[0]
    tile_len = tok_rows // tiles
    floats = whole.astype(jnp.float32)
    center = jnp.mean(floats, axis=-1, keepdims=True)
    spread = jnp.mean((floats - center) ** 2, axis=-1, keepdims=True)
    normed = ((floats - center) * lax.rsqrt(spread + 1e-06) * (1.0 + scale) + shift).astype(
        jnp.bfloat16
    )
    piece = lax.all_gather(w_qkv, "band", axis=0, tiled=True)
    rows_here = piece.shape[0]
    projected = jnp.dot(
        normed, piece.reshape(rows_here, 3 * head_feats), preferred_element_type=jnp.float32
    )
    projected = projected.reshape(tok_rows, 3, heads, head_size)
    queries = head_norm(projected[:, 0], q_gain)
    keys = head_norm(projected[:, 1], k_gain)
    values = projected[:, 2].astype(jnp.bfloat16)
    joined = jnp.concatenate(
        [keys.reshape(tok_rows, head_feats), values.reshape(tok_rows, head_feats)], axis=1
    )
    joined = joined.reshape(1, 1, tiles, tile_len, 2 * head_feats)
    extended = padded_2(joined, (("slab", 0), ("band", 1)), 1)
    padded = jnp.pad(extended, ((0, 0), (0, 0), (1, 1), (0, 0), (0, 0)))
    slab_pos = lax.axis_index("slab")
    band_pos = lax.axis_index("band")
    band_count = lax.axis_size("band")
    slot_ids = jnp.arange(tile_ids.shape[1], dtype=jnp.int32)
    query_tiles = queries.reshape(tiles, tile_len, heads, head_size)
    columns_all = jnp.arange(tiles, dtype=jnp.int32)
    flat_near = padded.reshape(9 * (tiles + 2), tile_len, 2 * head_feats)

    def one_tile(items):
        query, listed, number, column = items
        time_near = listed // (band_count * tiles)
        row_near = listed // tiles % band_count
        column_near = listed % tiles
        place = (
            ((time_near - slab_pos + 1) * 3 + (row_near - band_pos + 1)) * (tiles + 2)
            + column_near
            + 1
        )
        near = jnp.take(flat_near, place, axis=0)
        allowed = slot_ids < number
        return attend(query, near, allowed, head_feats, head_size)

    attended = lax.map(one_tile, (query_tiles, tile_ids, key_counts, columns_all))
    attended = attended.reshape(tok_rows, head_feats)
    product = jnp.dot(attended, w_out, preferred_element_type=jnp.float32)
    shares = lax.psum_scatter(
        product.astype(jnp.bfloat16), "tp", scatter_dimension=1, tiled=True
    ).astype(jnp.float32)
    return (gate * shares).astype(jnp.bfloat16)


def solution(mesh):
    in_specs = (
        P(("slab", "band"), "tp"),
        P("band", None, "tp"),
        P("tp", None),
        P(),
        P(),
        P("tp"),
        P(),
        P(),
        P(("slab", "band"), None),
        P(("slab", "band")),
    )
    out_specs = P(("slab", "band"), "tp")
    return jax.shard_map(shards, mesh=mesh, in_specs=in_specs, out_specs=out_specs, check_vma=False)
```

profile of v0, /device:TPU:0, one launch (start us, length us, event | category | flops | bytes accessed | tf_op | source)
XLA Modules:
  0.0 589.7 jit_solution(6342606409042847437)
XLA Ops:
  6.5 0.7 all-gather.3.cloned.1.call-update
  7.3 6.1 %copy.16 = bf16[768,3,768]{0,2,1:T(8,128)(2,1)} copy(bf16[768,3,768]{2,0,1:T(8,128)(2,1)} %param.13) | data formatting | bytes 7077888 | tf_op args[1]
  13.5 22.2 %all-gather.3.cloned.1.call-done = bf16[384,3072]{1,0:T(8,128)(2,1)} async-done(((bf16[384,768]{1,0:T(8,128)(2,1)}), bf16[384,3072]{1,0:T(8,128)(2,1)}) %all-gather.3.cloned.1.call-update) | async-done | bytes 2359312 | tf_op jit(solution)/shard_map/all_gather | solution.py:43
  35.7 2.2 convert_reduce_fusion
  37.9 2.4 fusion.58
  40.3 240.9 %all-gather.5.cloned.1.call-done = bf16[3072,3,768]{0,2,1:T(8,128)(2,1)} async-done(((bf16[768,3,768]{0,2,1:T(8,128)(2,1)}), bf16[3072,3,768]{0,2,1:T(8,128)(2,1)}) %all-gather.5.cloned.1.call-update) | async-done | bytes 14155792 | tf_op jit(solution)/shard_map/all_gather | solution.py:56
  281.2 9.4 %fusion.63 = f32[384,3,6,128]{3,0,2,1:T(8,128)S(1)} fusion(bf16[3,6,128,3072]{3,2,1,0:T(8,128)(2,1)} %bitcast.151, bf16[384,3072]{1,0:T(8,128)(2,1)S(1)} %copy-done.2, f32[3072]{0:T(1024)S(1)} %copy-done.7, f32[3072]{0:T(1024)S(1)} %broadcast_add_fusion, f32[384]{0:T(512)S(1)} %add_rsqrt_fusion.1, f32[384]{0:T(512)S(1)} %broadcast_multiply_fusion), kind=kOutput, calls=%fused_computation.85 | convolution fusion | flops 5442895872 | bytes 20081664 | tf_op jit(solution)/shard_map/dot_general | solution.py:58
  290.6 1.6 multiply_reduce_fusion
  293.2 2.0 copy.17
  295.2 1.3 squeeze.25
  297.6 1.5 multiply_convert_fusion.1
  299.2 3.5 collective-permute-start
  302.6 1.3 collective-permute-start.1
  303.9 24.0 %collective-permute-done = bf16[1,1,3,128,1536]{4,3,2,1,0:T(8,128)(2,1)S(1)} collective-permute-done((bf16[1,1,3,128,1536]{4,3,2,1,0:T(8,128)(2,1)S(1)}, bf16[1,1,3,128,1536]{4,3,2,1,0:T(8,128)(2,1)S(1)}, u32[]{:S(2)}, u32[]{:S(2)}) %collective-permute-start) | collective-permute-done | bytes 1179680 | tf_op jit(solution)/shard_map/ppermute | solution.py:12
  327.9 4.2 collective-permute-done.1
  332.1 1.9 pad_maximum_fusion
  334.0 3.0 collective-permute-start.2
  337.1 1.5 collective-permute-start.3
  338.6 2.5 fusion.70
  341.1 69.6 %collective-permute-done.2 = bf16[3,1,3,128,1536]{4,3,2,1,0:T(8,128)(2,1)} collective-permute-done((bf16[3,1,3,128,1536]{4,3,2,1,0:T(8,128)(2,1)}, bf16[3,1,3,128,1536]{4,3,2,1,0:T(8,128)(2,1)}, u32[]{:S(2)}, u32[]{:S(2)}) %collective-permute-start.2) | collective-permute-done | bytes 3538976 | tf_op jit(solution)/shard_map/ppermute | solution.py:12
  410.7 5.9 collective-permute-done.3
  416.6 9.2 %select_maximum_fusion = bf16[3,3,5,128,1536]{4,3,2,1,0:T(8,128)(2,1)} fusion(bf16[3,1,3,128,1536]{4,3,2,1,0:T(8,128)(2,1)} %collective-permute-done.3, bf16[3,1,3,128,1536]{4,3,2,1,0:T(8,128)(2,1)} %collective-permute-done.2, bf16[1,1,3,128,1536]{4,3,2,1,0:T(8,128)(2,1)S(1)} %collective-permute-done.1, ...), kind=kLoop, calls=%fused_computation.65 | loop fusion | flops 185794560 | bytes 28311552 | tf_op jit(solution)/shard_map/concatenate | solution.py:16
  425.8 119.3 %while.14 = (s32[]{:T(128)}, bf16[3,128,768]{2,1,0:T(8,128)(2,1)}, s32[3,14]{1,0:T(4,128)S(1)}, s32[]{:T(128)}, s32[]{:T(128)}, /*index=5*/bf16[45,128,1536]{2,1...) while((s32[]{:T(128)}, bf16[3,128,768]{2,1,0:T(8,128)(2,1)}, ...), condition=%wide.region_7.8_spmd.clone, body=%wide.region_4.7_spmd.clone.sunk | while | flops 715755456 | bytes 62667732 | solution.py:93
  425.8 9.4 %gather_fusion = bf16[14,128,1536]{2,1,0:T(8,128)(2,1)} fusion(bf16[45,128,1536]{2,1,0:T(8,128)(2,1)} %get-tuple-element.286, s32[1024]{0:T(1024)S(1)} %pad_clamp_fusion.2), kind=kCustom, calls=%fused_computation.clone.clone.1 | custom fusion | bytes 11010104 | tf_op jit(solution)/shard_map/while/body/eval_jaxpr/jit(_take)/gather | solution.py:89
  435.3 3.1 broadcast_select_fusion.2
  438.4 2.2 fusion.91
  440.6 6.7 %reshape.357 = bf16[1792,6,128]{2,1,0:T(8,128)(2,1)} reshape(bf16[14,128,768]{2,1,0:T(8,128)(2,1)} %get-tuple-element.259) | data formatting | bytes 5505024 | tf_op jit(solution)/shard_map/while/body/eval_jaxpr/reshape | solution.py:29
  448.7 6.7 %fusion.92 = (f32[6,128]{1,0:T(8,128)S(1)}, f32[6,128,1792]{2,1,0:T(8,128)}) fusion(pred[1792]{0:T(1024)(128)(4,1)S(1)} %broadcast_bitcast_fusion.3, bf16[1792,6,128]{2,1,0:T(8,128)(2,1)} %reshape.357, bf16[3,128,6,128]{3,1,2,0:T(8,128)(2,1)} %get-tuple-element.288, s32[]{:T(128)} %get-tuple-element.272), kind=kOutput, calls=%fused_computation.106.clone.1 | convolution fusion | flops 357828352 | bytes 9377024 | tf_op jit(solution)/shard_map/while/body/eval_jaxpr/sub | solution.py:36
  455.4 4.2 reshape.358
  459.6 5.1 fusion.93
  464.8 0.7 constant_dynamic-update-slice_fusion.2
  465.6 9.4 %gather_fusion = bf16[14,128,1536]{2,1,0:T(8,128)(2,1)} fusion(bf16[45,128,1536]{2,1,0:T(8,128)(2,1)} %get-tuple-element.286, s32[1024]{0:T(1024)S(1)} %pad_clamp_fusion.2), kind=kCustom, calls=%fused_computation.clone.clone.1 | custom fusion | bytes 11010104 | tf_op jit(solution)/shard_map/while/body/eval_jaxpr/jit(_take)/gather | solution.py:89
  475.0 3.1 broadcast_select_fusion.2
  478.2 2.2 fusion.91
  480.4 6.7 %reshape.357 = bf16[1792,6,128]{2,1,0:T(8,128)(2,1)} reshape(bf16[14,128,768]{2,1,0:T(8,128)(2,1)} %get-tuple-element.259) | data formatting | bytes 5505024 | tf_op jit(solution)/shard_map/while/body/eval_jaxpr/reshape | solution.py:29
  488.5 6.7 %fusion.92 = (f32[6,128]{1,0:T(8,128)S(1)}, f32[6,128,1792]{2,1,0:T(8,128)}) fusion(pred[1792]{0:T(1024)(128)(4,1)S(1)} %broadcast_bitcast_fusion.3, bf16[1792,6,128]{2,1,0:T(8,128)(2,1)} %reshape.357, bf16[3,128,6,128]{3,1,2,0:T(8,128)(2,1)} %get-tuple-element.288, s32[]{:T(128)} %get-tuple-element.272), kind=kOutput, calls=%fused_computation.106.clone.1 | convolution fusion | flops 357828352 | bytes 9377024 | tf_op jit(solution)/shard_map/while/body/eval_jaxpr/sub | solution.py:36
  495.2 4.2 reshape.358
  499.4 5.1 fusion.93
  505.4 9.4 %gather_fusion = bf16[14,128,1536]{2,1,0:T(8,128)(2,1)} fusion(bf16[45,128,1536]{2,1,0:T(8,128)(2,1)} %get-tuple-element.286, s32[1024]{0:T(1024)S(1)} %pad_clamp_fusion.2), kind=kCustom, calls=%fused_computation.clone.clone.1 | custom fusion | bytes 11010104 | tf_op jit(solution)/shard_map/while/body/eval_jaxpr/jit(_take)/gather | solution.py:89
  514.8 3.1 broadcast_select_fusion.2
  518.0 2.2 fusion.91
  520.1 6.7 %reshape.357 = bf16[1792,6,128]{2,1,0:T(8,128)(2,1)} reshape(bf16[14,128,768]{2,1,0:T(8,128)(2,1)} %get-tuple-element.259) | data formatting | bytes 5505024 | tf_op jit(solution)/shard_map/while/body/eval_jaxpr/reshape | solution.py:29
  528.2 6.7 %fusion.92 = (f32[6,128]{1,0:T(8,128)S(1)}, f32[6,128,1792]{2,1,0:T(8,128)}) fusion(pred[1792]{0:T(1024)(128)(4,1)S(1)} %broadcast_bitcast_fusion.3, bf16[1792,6,128]{2,1,0:T(8,128)(2,1)} %reshape.357, bf16[3,128,6,128]{3,1,2,0:T(8,128)(2,1)} %get-tuple-element.288, s32[]{:T(128)} %get-tuple-element.272), kind=kOutput, calls=%fused_computation.106.clone.1 | convolution fusion | flops 357828352 | bytes 9377024 | tf_op jit(solution)/shard_map/while/body/eval_jaxpr/sub | solution.py:36
  534.9 4.2 reshape.358
  539.1 5.1 fusion.93
  545.1 6.0 %convolution_convert_fusion = bf16[384,3072]{1,0:T(8,128)(2,1)} fusion(bf16[384,768]{1,0:T(8,128)(2,1)} %bitcast.152, bf16[768,3072]{1,0:T(8,128)(2,1)} %param.14), kind=kOutput, calls=%fused_computation.82 | convolution fusion | flops 1813118976 | bytes 7667712 | tf_op jit(solution)/shard_map/dot_general | solution.py:95
  551.1 30.2 %reduce-scatter.2.cloned.1.call-done = bf16[384,768]{1,0:T(8,128)(2,1)} async-done(((bf16[384,3072]{1,0:T(8,128)(2,1)}), bf16[384,768]{1,0:T(8,128)(2,1)}) %reduce-scatter.2.cloned.1.call-update) | async-done | bytes 589840 | tf_op jit(solution)/shard_map/reduce_scatter | solution.py:96
  581.2 2.0 multiply_convert_fusion
  (60 shorter events, 8.6 us)
Async XLA Ops:
  6.5 6.9 %copy-start = (f32[128]{0:T(128)S(1)}, f32[128]{0:T(128)}, u32[]{:S(2)}) copy-start(f32[128]{0:T(128)} %param.19) | copy-start | bytes 1540
  6.5 29.2 %all-gather.3.cloned.1.call-start = ((), (), s32[]{:S(2)}) async-start(), calls=%async_computation.1 | async-start | bytes 2949120 | tf_op jit(solution)/shard_map/all_gather | solution.py:43
  7.3 6.2 %copy-start.4 = (f32[3072]{0:T(1024)S(1)}, f32[3072]{0:T(1024)}, u32[]{:S(2)}) copy-start(f32[3072]{0:T(1024)} %param.16) | copy-start | bytes 36868
  7.3 273.9 %all-gather.5.cloned.1.call-start = ((), (), s32[]{:S(2)}) async-start(), calls=%async_computation.2 | async-start | bytes 17694720 | tf_op jit(solution)/shard_map/all_gather | solution.py:56
  13.4 267.8 %copy-start.7 = (f32[3072]{0:T(1024)S(1)}, f32[3072]{0:T(1024)}, u32[]{:S(2)}) copy-start(f32[3072]{0:T(1024)} %param.15) | copy-start | bytes 36868
  13.4 567.8 %reduce-scatter.2.cloned.1.call-start = ((), (), s32[]{:S(2)}) async-start(), calls=%async_computation.3 | async-start | bytes 2949120 | tf_op jit(solution)/shard_map/reduce_scatter | solution.py:96
  35.7 245.5 %copy-start.2 = (bf16[384,3072]{1,0:T(8,128)(2,1)S(1)}, bf16[384,3072]{1,0:T(8,128)(2,1)}, u32[]{:S(2)}) copy-start(bf16[384,3072]{1,0:T(8,128)(2,1)} %all-gather.3.cloned.1.call-done) | copy-start | bytes 7077892
  299.1 39.5 %copy-start.6 = (f32[128]{0:T(128)S(1)}, f32[128]{0:T(128)}, u32[]{:S(2)}) copy-start(f32[128]{0:T(128)} %param.18) | copy-start | bytes 1540
  299.2 28.8 %collective-permute-start = (bf16[1,1,3,128,1536]{4,3,2,1,0:T(8,128)(2,1)S(1)}, bf16[1,1,3,128,1536]{4,3,2,1,0:T(8,128)(2,1)S(1)}, u32[]{:S(2)}, u32[]{:S(2)}) collective-permute-start(bf16[1,1,3,128,1536]{4,3,2,1,0:T(8,128)(2,1)S(1)} %pad_maximum_fusion.1), channel_id=1, source_target_pairs={{0,16},{1,17},{2,18},{3,19},{4,20},{5,21},{6,22},{7,23},{8,24},{9,... | collective-permute-start | bytes 3538952 | tf_op jit(solution)/shard_map/ppermute | solution.py:12
  302.6 29.5 %collective-permute-start.1 = (bf16[1,1,3,128,1536]{4,3,2,1,0:T(8,128)(2,1)S(1)}, bf16[1,1,3,128,1536]{4,3,2,1,0:T(8,128)(2,1)S(1)}, u32[]{:S(2)}, u32[]{:S(2)}) collective-permute-start(bf16[1,1,3,128,1536]{4,3,2,1,0:T(8,128)(2,1)S(1)} %pad_maximum_fusion.1), channel_id=1, source_target_pairs={{16,0},{17,1},{18,2},{19,3},{20,4},{21,5},{22,6},{23,7},{24,8},{25... | collective-permute-start | bytes 3538952 | tf_op jit(solution)/shard_map/ppermute | solution.py:15
  334.0 76.7 %collective-permute-start.2 = (bf16[3,1,3,128,1536]{4,3,2,1,0:T(8,128)(2,1)}, bf16[3,1,3,128,1536]{4,3,2,1,0:T(8,128)(2,1)}, u32[]{:S(2)}, u32[]{:S(2)}) collective-permute-start(bf16[3,1,3,128,1536]{4,3,2,1,0:T(8,128)(2,1)} %pad_maximum_fusion), channel_id=1, source_target_pairs={{0,1},{1,2},{2,3},{4,5},{5,6},{6,7},{8,9},{9,10},{10,11},{12,13},{... | collective-permute-start | bytes 10616840 | tf_op jit(solution)/shard_map/ppermute | solution.py:12
  337.1 79.5 %collective-permute-start.3 = (bf16[3,1,3,128,1536]{4,3,2,1,0:T(8,128)(2,1)}, bf16[3,1,3,128,1536]{4,3,2,1,0:T(8,128)(2,1)}, u32[]{:S(2)}, u32[]{:S(2)}) collective-permute-start(bf16[3,1,3,128,1536]{4,3,2,1,0:T(8,128)(2,1)} %pad_maximum_fusion), channel_id=1, source_target_pairs={{1,0},{2,1},{3,2},{5,4},{6,5},{7,6},{9,8},{10,9},{11,10},{13,12},{... | collective-permute-start | bytes 10616840 | tf_op jit(solution)/shard_map/ppermute | solution.py:15
  341.1 84.7 %copy-start.3 = (s32[3,14]{1,0:T(4,128)S(1)}, s32[3,14]{1,0:T(4,128)}, u32[]{:S(2)}) copy-start(s32[3,14]{1,0:T(4,128)} %param.20) | copy-start | bytes 508
  341.1 84.7 %copy-start.8 = (s32[3]{0:T(128)S(1)}, s32[3]{0:T(128)}, u32[]{:S(2)}) copy-start(s32[3]{0:T(128)} %param.21) | copy-start | bytes 40
  545.1 36.2 %copy-start.5 = (f32[768]{0:T(1024)S(1)}, f32[768]{0:T(1024)}, u32[]{:S(2)}) copy-start(f32[768]{0:T(1024)} %param.17) | copy-start | bytes 9220
  545.1 38.1 %copy-start.1 = (f32[128]{0:T(128)S(1)}, f32[128]{0:T(128)}, u32[]{:S(2)}) copy-start(f32[128]{0:T(128)} %param.19) | copy-start | bytes 1540
Sparse Core Ops, SparseCore 0:
  8.9 26.7 all-gather.2
  37.3 243.8 all-gather.4
  551.2 30.0 reduce-scatter.1
where the time goes:
time: 591 us; the launch traced here: 590 us
  waiting for transfers between devices  398 us (67%)
  local copies, waits for them, and re-layouts  83.5 us (14%)
  matrix products  50.7 us (9%)
  other arithmetic  35.2 us (6%)
  between operations  13.3 us (2%)
  starting transfers between devices  9.33 us (2%)
    all_gather x1, waiting for transfers between devices, shards(): piece = lax.all_gather(w_qkv, 'band', axis=0, tiled=True)  241 us
    ppermute x2, waiting for transfers between devices, padded_2(): lax.ppermute(lax.slice_in_dim(block, block.shape[dim] - width, None, axis...  93.6 us
    reduce_scatter x1, waiting for transfers between devices, shards(): lax.psum_scatter(product.astype(jnp.bfloat16), 'tp', scatter_dimension=1,...  30.2 us
    gather x3, local copies, waits for them, and re-layouts, one_tile(): near = jnp.take(flat_near, place, axis=0)  28.2 us
    all_gather x1, waiting for transfers between devices, shards(): whole = lax.all_gather(tokens, 'tp', axis=1, tiled=True)  22.2 us
    sub x3, matrix products, attend(): weights = jnp.exp(scores - top)  20.1 us
    reshape x3, local copies, waits for them, and re-layouts, attend(): near[:, :, :head_feats].reshape(many * tile_len, heads, head_size)  20 us
    dot_general x3, matrix products, attend(): jnp.einsum('hqk,khd->qhd', probs, near_values, preferred_element_type=jnp...  15.3 us
  transfers between devices with their start and end apart: 7, of which 7 were waited for; matrix products, arithmetic and copies ran while one was open for 2% of the time, Pallas kernels for 0%

commit v1 on v0

v1 whole, which is shorter than its diff:
```python
import functools

import jax
import jax.numpy as jnp
from jax import lax
from jax.experimental import pallas as pl
from jax.experimental.pallas import tpu as pltpu
from jax.sharding import PartitionSpec as P

BF = jnp.bfloat16
F32 = jnp.float32


def proj_kernel(normalize, head_size, x_ref, scale_ref, shift_ref, w_ref, gain_ref, o_ref, normed):
    part = pl.program_id(1)

    @pl.when(part == 0)
    def _():
        floats = x_ref[...].astype(F32)
        center = jnp.mean(floats, axis=-1, keepdims=True)
        moved = floats - center
        spread = jnp.mean(moved * moved, axis=-1, keepdims=True)
        normed[...] = (
            moved * lax.rsqrt(spread + 1e-06) * (1.0 + scale_ref[...]) + shift_ref[...]
        ).astype(BF)

    product = jnp.dot(normed[...], w_ref[...], preferred_element_type=F32)

    def write(normed_part):
        for head in range(product.shape[1] // head_size):
            cols = slice(head * head_size, (head + 1) * head_size)
            piece = product[:, cols]
            if normed_part:
                squares = jnp.mean(piece * piece, axis=-1, keepdims=True)
                piece = piece * lax.rsqrt(squares + 1e-06) * gain_ref[...]
            o_ref[:, cols] = piece.astype(BF)

    if all(normalize):
        write(True)
    else:

        @pl.when(part == 0)
        def _():
            write(True)

        @pl.when(part != 0)
        def _():
            write(False)


def project(x, scale, shift, w, gain, normalize):
    rows, width = x.shape
    parts = len(normalize)
    cols = w.shape[1] // parts
    block = 256 if rows % 256 == 0 else rows
    return pl.pallas_call(
        functools.partial(proj_kernel, normalize, gain.shape[0]),
        grid=(rows // block, parts),
        in_specs=[
            pl.BlockSpec((block, width), lambda i, j: (i, 0)),
            pl.BlockSpec((1, width), lambda i, j: (0, 0)),
            pl.BlockSpec((1, width), lambda i, j: (0, 0)),
            pl.BlockSpec((width, cols), lambda i, j: (0, j)),
            pl.BlockSpec((1, gain.shape[0]), lambda i, j: (0, 0)),
        ],
        out_specs=pl.BlockSpec((block, cols), lambda i, j: (i, j)),
        out_shape=jax.ShapeDtypeStruct((rows, parts * cols), BF),
        scratch_shapes=[pltpu.VMEM((block, width), BF)],
        cost_estimate=pl.CostEstimate(
            flops=2 * rows * width * parts * cols,
            bytes_accessed=2 * (rows * width + width * parts * cols + rows * parts * cols),
            transcendentals=0,
        ),
        name="project",
    )(x, scale.reshape(1, -1), shift.reshape(1, -1), w, gain.reshape(1, -1))


def attend_kernel(head_size, place_ref, count_ref, q_ref, kv_ref, o_ref, sc):
    tile = pl.program_id(0)
    tile_len, feats = q_ref.shape
    heads = feats // head_size
    count = count_ref[tile]
    trips = (count + 1) // 2
    inverse = 1.0 / head_size**0.5
    lane = lax.broadcasted_iota(jnp.int32, (tile_len, 2 * tile_len), 1)

    def near(j, first, head):
        cols = slice(first + head * head_size, first + (head + 1) * head_size)
        one = kv_ref[place_ref[tile, 2 * j], :, cols]
        two = kv_ref[place_ref[tile, 2 * j + 1], :, cols]
        return jnp.concatenate([one, two], axis=0)

    def score(j, tops):
        limit = (count - 2 * j) * tile_len
        out = []
        for head in range(heads):
            query = q_ref[:, head * head_size : (head + 1) * head_size]
            scores = lax.dot_general(
                query, near(j, 0, head), (((1,), (1,)), ((), ())), preferred_element_type=F32
            )
            scores = jnp.where(lane < limit, scores * inverse, -1e30)
            sc[j, head] = scores
            out.append(jnp.maximum(tops[head], scores))
        return tuple(out)

    low = jnp.full((tile_len, 2 * tile_len), -1e30, F32)
    tops = lax.fori_loop(0, trips, score, (low,) * heads)
    tops = [jnp.max(top, axis=-1, keepdims=True) for top in tops]

    def weigh(j, sums):
        out = []
        for head in range(heads):
            weights = jnp.exp(sc[j, head] - tops[head])
            sc[j, head] = weights
            out.append(sums[head] + weights)
        return tuple(out)

    sums = lax.fori_loop(0, trips, weigh, (jnp.zeros((tile_len, 2 * tile_len), F32),) * heads)
    shares = [1.0 / jnp.sum(total, axis=-1, keepdims=True) for total in sums]

    def gather(j, totals):
        out = []
        for head in range(heads):
            probs = (sc[j, head] * shares[head]).astype(BF)
            out.append(
                totals[head] + jnp.dot(probs, near(j, feats, head), preferred_element_type=F32)
            )
        return tuple(out)

    totals = lax.fori_loop(0, trips, gather, (jnp.zeros((tile_len, head_size), F32),) * heads)
    for head in range(heads):
        o_ref[:, head * head_size : (head + 1) * head_size] = totals[head].astype(BF)


def attention(place, counts, queries, keys_values, head_size):
    tiles, slots = place.shape
    rows, feats = queries.shape
    tile_len = rows // tiles
    heads = feats // head_size
    many = keys_values.shape[0]
    if slots % 2:
        place = jnp.pad(place, ((0, 0), (0, 1)))
    return pl.pallas_call(
        functools.partial(attend_kernel, head_size),
        grid_spec=pltpu.PrefetchScalarGridSpec(
            num_scalar_prefetch=2,
            grid=(tiles,),
            in_specs=[
                pl.BlockSpec((tile_len, feats), lambda i, a, b: (i, 0)),
                pl.BlockSpec((many, tile_len, 2 * feats), lambda i, a, b: (0, 0, 0)),
            ],
            out_specs=pl.BlockSpec((tile_len, feats), lambda i, a, b: (i, 0)),
            scratch_shapes=[pltpu.VMEM(((slots + 1) // 2, heads, tile_len, 2 * tile_len), F32)],
        ),
        out_shape=jax.ShapeDtypeStruct((rows, feats), BF),
        cost_estimate=pl.CostEstimate(
            flops=4 * rows * slots * tile_len * feats,
            bytes_accessed=2 * (2 * rows * feats + many * tile_len * 2 * feats),
            transcendentals=rows * slots * tile_len * heads,
        ),
        name="attend",
    )(place, counts, queries, keys_values)


def shards(tokens, w_qkv, w_out, shift, scale, gate, q_gain, k_gain, tile_ids, key_counts):
    slabs, bands = lax.axis_size("slab"), lax.axis_size("band")
    slab_pos, band_pos = lax.axis_index("slab"), lax.axis_index("band")
    parity = slab_pos % 2
    tok_rows = tokens.shape[0]
    head_feats = w_out.shape[0]
    half = head_feats // 2
    head_size = q_gain.shape[0]
    tiles = key_counts.shape[0]
    tile_len = tok_rows // tiles
    swap = [(i, i ^ 1) for i in range(slabs)]

    other = lax.ppermute(tokens, "slab", swap)
    whole = lax.all_gather(jnp.concatenate([tokens, other], axis=0), "tp", axis=1, tiled=True)
    lists = jnp.concatenate([tile_ids, key_counts[:, None]], axis=1)
    lists = jnp.concatenate([lists, lax.ppermute(lists, "slab", swap)], axis=0)
    ids, counts = lists[:, :-1], lists[:, -1]

    mine = lax.dynamic_slice_in_dim(w_qkv, parity * half, half, axis=2)
    depth = mine.shape[0]
    w_kv = lax.all_gather(mine[:, 1:].reshape(depth, 2 * half), "band", axis=0, tiled=True)
    w_q = lax.all_gather(mine[:, 0].reshape(depth, half), "band", axis=0, tiled=True)

    joined = project(whole, scale, shift, w_kv, k_gain, (True, False))
    joined = joined.reshape(2, tiles, tile_len, 2 * half)
    if slabs > 2:
        first = jnp.where(parity == 0, joined[0], joined[1])
        second = jnp.where(parity == 0, joined[1], joined[0])
        up = [(i, i + 2) for i in range(slabs - 2)]
        below = lax.ppermute(second, "slab", up)
        above = lax.ppermute(first, "slab", [(b, a) for a, b in up])
        joined = jnp.concatenate([joined, below[None], above[None]], axis=0)
    groups = joined.shape[0]
    forward = [(i, i + 1) for i in range(bands - 1)]
    left = lax.ppermute(joined, "band", forward)
    right = lax.ppermute(joined, "band", [(b, a) for a, b in forward])
    queries = project(whole, scale, shift, w_q, q_gain, (True,))
    near = jnp.concatenate([left, joined, right], axis=0)
    near = near.reshape(3 * groups * tiles, tile_len, 2 * half)

    time_near = ids // (bands * tiles) - (slab_pos - parity)
    group = jnp.where(
        time_near < 0, 2, jnp.where(time_near > 1, 3, jnp.where(time_near == parity, 0, 1))
    )
    row_near = ids // tiles % bands - band_pos + 1
    place = (row_near * groups + group) * tiles + ids % tiles

    attended = attention(place, counts, queries, near, head_size)
    back = lax.ppermute(attended[tok_rows:], "slab", swap)
    ours = attended[:tok_rows]
    joint = jnp.where(
        parity == 0,
        jnp.concatenate([ours, back], axis=1),
        jnp.concatenate([back, ours], axis=1),
    )
    product = jnp.dot(joint, w_out, preferred_element_type=F32)
    shares = lax.psum_scatter(
        product.astype(BF), "tp", scatter_dimension=1, tiled=True
    ).astype(F32)
    return (gate * shares).astype(BF)


def solution(mesh):
    in_specs = (
        P(("slab", "band"), "tp"),
        P("band", None, "tp"),
        P("tp", None),
        P(),
        P(),
        P("tp"),
        P(),
        P(),
        P(("slab", "band"), None),
        P(("slab", "band")),
    )
    out_specs = P(("slab", "band"), "tp")
    return jax.shard_map(shards, mesh=mesh, in_specs=in_specs, out_specs=out_specs, check_vma=False)
```

time: 591 us -> 307 us (0.52)
  waiting for transfers between devices: 398 us -> 220 us
  local copies, waits for them, and re-layouts: 83.5 us -> 6.94 us
  matrix products: 50.7 us -> 6.18 us
  Pallas kernels: 0 us -> 37.6 us
  other arithmetic: 35.2 us -> 8.32 us
    all_gather x2 -> x3, waiting for transfers between devices: 263 us -> 155 us  [the longest x1 72.4 us: shards(): lax.all_gather(mine[:, 1:].reshape(depth, 2 * half), 'band', axis=0, tile...]
    ppermute x4 -> x5, waiting for transfers between devices: 104 us -> 23.2 us  [the longest x1 13.5 us: shards(): other = lax.ppermute(tokens, 'slab', swap)]
    pallas_call x0 -> x3, Pallas kernels: none -> 37.6 us  [the longest x2 24.2 us: project(): pl.pallas_call(functools.partial(proj_kernel, normalize, gain.shape[0]),...]
    reshape x6 -> x1, local copies, waits for them, and re-layouts: 32.6 us -> 1.19 us  [shards(): mine[:, 1:].reshape(depth, 2 * half)]
    gather x3 -> x0, local copies, waits for them, and re-layouts: 28.2 us -> none  [one_tile(): near = jnp.take(flat_near, place, axis=0)]
    dot_general x5 -> x1, matrix products: 30.6 us -> 6.18 us  [shards(): product = jnp.dot(joint, w_out, preferred_element_type=F32)]
    sub x3 -> x0, matrix products: 20.1 us -> none  [attend(): weights = jnp.exp(scores - top)]
    reduce_scatter x1, waiting for transfers between devices: 30.2 us -> 41.4 us  [shards(): lax.psum_scatter(product.astype(BF), 'tp', scatter_dimension=1, tiled=True)]
  transfers between devices with their start and end apart: 7 -> 9, of which waited for: 7 -> 7; matrix products, arithmetic and copies ran while one was open for 2% -> 2% of each run, Pallas kernels for 0% -> 8%
where the time goes in v1:
time: 307 us; the launch traced here: 305 us
  waiting for transfers between devices  220 us (72%)
  Pallas kernels  37.6 us (12%)
  between operations  13.2 us (4%)
  starting transfers between devices  13.1 us (4%)
  other arithmetic  8.32 us (3%)
  local copies, waits for them, and re-layouts  6.94 us (2%)
  matrix products  6.18 us (2%)
    all_gather x1, waiting for transfers between devices, shards(): lax.all_gather(mine[:, 1:].reshape(depth, 2 * half), 'band', axis=0, tile...  72.4 us
    all_gather x1, waiting for transfers between devices, shards(): lax.all_gather(mine[:, 0].reshape(depth, half), 'band', axis=0, tiled=True)  45.6 us
    reduce_scatter x1, waiting for transfers between devices, shards(): lax.psum_scatter(product.astype(BF), 'tp', scatter_dimension=1, tiled=True)  41.4 us
    all_gather x1, waiting for transfers between devices, shards(): lax.all_gather(jnp.concatenate([tokens, other], axis=0), 'tp', axis=1, ti...  37.4 us
    pallas_call x2, Pallas kernels, project(): pl.pallas_call(functools.partial(proj_kernel, normalize, gain.shape[0]),...  24.2 us
    ppermute x1, waiting for transfers between devices, shards(): other = lax.ppermute(tokens, 'slab', swap)  13.5 us
    pallas_call x1, Pallas kernels, attention(): pl.pallas_call(functools.partial(attend_kernel, head_size), grid_spec=plt...  13.4 us
    ppermute x1, waiting for transfers between devices, shards(): back = lax.ppermute(attended[tok_rows:], 'slab', swap)  7.61 us
  transfers between devices with their start and end apart: 9, of which 7 were waited for; matrix products, arithmetic and copies ran while one was open for 2% of the time, Pallas kernels for 8%

profile of v1, /device:TPU:0, one launch (start us, length us, event | category | flops | bytes accessed | tf_op | source)
XLA Modules:
  0.0 305.5 jit_solution(3975020158332398825)
XLA Ops:
  6.5 0.0 copy-start
  6.5 0.0 all-gather.7.cloned.1.call-start
  6.5 2.0 copy-done
  8.5 0.1 dynamic-slice_bitcast_fusion
  8.7 1.2 copy.15
  9.8 0.0 all-gather.7.cloned.1.call-update
  9.9 0.0 all-gather.5.cloned.1.call-start
  9.9 3.1 %collective-permute-start.1 = (bf16[384,768]{1,0:T(8,128)(2,1)}, bf16[384,768]{1,0:T(8,128)(2,1)S(1)}, u32[]{:S(2)}, u32[]{:S(2)}) collective-permute-start(bf16[384,768]{1,0:T(8,128)(2,1)} %param.10), channel_id=1, source_target_pairs={{0,16},{16,0},{1,17},{17,1},{2,18},{18,2},{3,19},{19,3},{4,20},{20... | collective-permute-start | bytes 1769480 | tf_op jit(solution)/shard_map/ppermute | solution.py:177
  13.0 13.5 %collective-permute-done.1 = bf16[384,768]{1,0:T(8,128)(2,1)S(1)} collective-permute-done((bf16[384,768]{1,0:T(8,128)(2,1)}, bf16[384,768]{1,0:T(8,128)(2,1)S(1)}, u32[]{:S(2)}, u32[]{:S(2)}) %collective-permute-start.1) | collective-permute-done | bytes 589856 | tf_op jit(solution)/shard_map/ppermute | solution.py:177
  26.5 2.1 pad_maximum_fusion.1
  28.7 0.0 all-gather.5.cloned.1.call-update
  28.7 0.0 all-gather.9.cloned.1.call-start
  28.7 0.9 constant_dynamic-slice_fusion
  29.6 0.0 all-gather.9.cloned.1.call-update
  29.6 0.0 reduce-scatter.2.cloned.1.call-start
  29.7 72.4 %all-gather.7.cloned.1.call-done.w_ref = bf16[3072,768]{1,0:T(8,128)(2,1)} async-done(((bf16[768,768]{1,0:T(8,128)(2,1)}), bf16[3072,768]{1,0:T(8,128)(2,1)}) %all-gather.7.cloned.1.call-update) | async-done | bytes 4718608 | tf_op jit(solution)/shard_map/all_gather | solution.py:185
  102.1 37.4 %all-gather.5.cloned.1.call-done.x_ref = bf16[768,3072]{1,0:T(8,128)(2,1)} async-done(((bf16[768,768]{1,0:T(8,128)(2,1)}), bf16[768,3072]{1,0:T(8,128)(2,1)}) %all-gather.5.cloned.1.call-update) | async-done | bytes 4718608 | tf_op jit(solution)/shard_map/all_gather | solution.py:178
  139.6 0.0 copy-start.3
  139.6 0.0 copy-start.1
  139.6 15.7 %project.3 = bf16[768,768]{1,0:T(8,128)(2,1)} custom-call(bf16[768,3072]{1,0:T(8,128)(2,1)} %all-gather.5.cloned.1.call-done.x_ref, f32[1,3072]{1,0:T(1,128)} %bitcast.18, f32[1,3072]{1,0:T(1,128)} %bitcast.20, bf16[3072,768]{1,0:T(8,128)(2,1)} %all-gather.7.cloned.1.call-done.w_ref, f32[1,128]{1,0:T(1,128)} %bitcast.24), custom_call_target="tpu_custom_call" | custom-call | flops 3623878656 | bytes 10616832 | tf_op jit(solution)/shard_map/project/pallas_call | solution.py:56
  155.3 1.3 collective-permute-start.3
  156.6 5.6 %collective-permute-start.2 = (bf16[2,3,128,768]{3,2,1,0:T(8,128)(2,1)}, bf16[2,3,128,768]{3,2,1,0:T(8,128)(2,1)}, u32[]{:S(2)}, u32[]{:S(2)}) collective-permute-start(bf16[2,3,128,768]{3,2,1,0:T(8,128)(2,1)} %bitcast.16), channel_id=1, source_target_pairs={{0,1},{1,2},{2,3},{4,5},{5,6},{6,7},{8,9},{9,10},{10,11},{12,13},{... | collective-permute-start | bytes 3538952 | tf_op jit(solution)/shard_map/ppermute | solution.py:199
  162.2 0.0 copy-done.3
  162.2 0.1 copy.13
  162.3 0.0 copy-done.1
  162.3 0.1 pad_add_fusion.1
  162.3 1.5 collective-permute-start
  163.8 2.1 collective-permute-done
  165.9 0.1 pad_add_fusion
  166.0 0.7 slice_reduce_fusion.count_ref
  166.7 0.6 fusion.12.place_ref
  167.3 45.6 %all-gather.9.cloned.1.call-done = bf16[3072,1,384]{2,0,1:T(8,128)(2,1)} async-done(((bf16[768,1,384]{2,0,1:T(8,128)(2,1)}), bf16[3072,1,384]{2,0,1:T(8,128)(2,1)}) %all-gather.9.cloned.1.call-update) | async-done | bytes 2359312 | tf_op jit(solution)/shard_map/all_gather | solution.py:186
  212.9 8.5 %project.2.q_ref = bf16[768,384]{1,0:T(8,128)(2,1)} custom-call(bf16[768,3072]{1,0:T(8,128)(2,1)} %all-gather.5.cloned.1.call-done.x_ref, f32[1,3072]{1,0:T(1,128)} %bitcast.19, f32[1,3072]{1,0:T(1,128)} %bitcast.21, bf16[3072,384]{1,0:T(8,128)(2,1)} %bitcast.14, f32[1,128]{1,0:T(1,128)} %bitcast.22), custom_call_target="tpu_custom_call" | custom-call | flops 1811939328 | bytes 7667712 | tf_op jit(solution)/shard_map/project/pallas_call | solution.py:56
  221.5 0.0 collective-permute-done.3
  221.5 0.0 collective-permute-done.2
  221.5 3.4 %pad_maximum_fusion = bf16[6,3,128,768]{3,2,1,0:T(8,128)(2,1)} fusion(bf16[2,3,128,768]{3,2,1,0:T(8,128)(2,1)} %collective-permute-done.3, bf16[2,3,128,768]{3,2,1,0:T(8,128)(2,1)} %bitcast.17, bf16[2,3,128,768]{3,2,1,0:T(8,128)(2,1)} %collective-permute-done.2), kind=kLoop, calls=%fused_computation.1 | loop fusion | flops 3538944 | bytes 7077888 | tf_op jit(solution)/shard_map/concatenate | solution.py:202
  224.9 13.4 %attend.1 = bf16[768,384]{1,0:T(8,128)(2,1)} custom-call(s32[6,14]{1,0:T(8,128)} %fusion.12.place_ref, s32[6]{0:T(128)} %slice_reduce_fusion.count_ref, bf16[768,384]{1,0:T(8,128)(2,1)} %project.2.q_ref, bf16[18,128,768]{2,1,0:T(8,128)(2,1)} %bitcast.13), custom_call_target="tpu_custom_call" | custom-call | flops 2113929216 | bytes 4718592 | tf_op jit(solution)/shard_map/attend/pallas_call | solution.py:143
  238.3 1.9 fusion.16
  240.2 1.6 collective-permute-start.4
  241.8 7.6 %collective-permute-done.4 = bf16[384,384]{1,0:T(8,128)(2,1)} collective-permute-done((bf16[384,384]{1,0:T(8,128)(2,1)}, bf16[384,384]{1,0:T(8,128)(2,1)}, u32[]{:S(2)}, u32[]{:S(2)}) %collective-permute-start.4) | collective-permute-done | bytes 294944 | tf_op jit(solution)/shard_map/ppermute | solution.py:213
  249.4 6.2 %convolution_convert_fusion = bf16[384,3072]{1,0:T(8,128)(2,1)} fusion(bf16[768,3072]{1,0:T(8,128)(2,1)} %param.12, bf16[384,384]{1,0:T(8,128)(2,1)} %collective-permute-done.4, bf16[384,384]{1,0:T(8,128)(2,1)} %get-tuple-element.5, pred[]{:T(512)S(6)} %eq.14), kind=kOutput, calls=%fused_computation | convolution fusion | flops 1815773184 | bytes 7667713 | tf_op jit(solution)/shard_map/dot_general | solution.py:220
  255.6 0.0 copy-start.2
  255.6 0.0 reduce-scatter.2.cloned.1.call-update
  255.6 41.4 %reduce-scatter.2.cloned.1.call-done = bf16[384,768]{1,0:T(8,128)(2,1)} async-done(((bf16[384,3072]{1,0:T(8,128)(2,1)}), bf16[384,768]{1,0:T(8,128)(2,1)}) %reduce-scatter.2.cloned.1.call-update) | async-done | bytes 589840 | tf_op jit(solution)/shard_map/reduce_scatter | solution.py:221
  296.9 0.0 copy-done.2
  296.9 2.0 multiply_convert_fusion
Async XLA Ops:
  6.5 2.0 copy-start
  6.5 95.6 %all-gather.7.cloned.1.call-start = ((), (), s32[]{:S(2)}) async-start(), calls=%async_computation.2 | async-start | bytes 5898240 | tf_op jit(solution)/shard_map/all_gather | solution.py:185
  9.9 129.7 %all-gather.5.cloned.1.call-start = ((), (), s32[]{:S(2)}) async-start(), calls=%async_computation.1 | async-start | bytes 5898240 | tf_op jit(solution)/shard_map/all_gather | solution.py:178
  9.9 16.6 %collective-permute-start.1 = (bf16[384,768]{1,0:T(8,128)(2,1)}, bf16[384,768]{1,0:T(8,128)(2,1)S(1)}, u32[]{:S(2)}, u32[]{:S(2)}) collective-permute-start(bf16[384,768]{1,0:T(8,128)(2,1)} %param.10), channel_id=1, source_target_pairs={{0,16},{16,0},{1,17},{17,1},{2,18},{18,2},{3,19},{19,3},{4,20},{20... | collective-permute-start | bytes 1769480 | tf_op jit(solution)/shard_map/ppermute | solution.py:177
  28.7 184.3 %all-gather.9.cloned.1.call-start = ((), (), s32[]{:S(2)}) async-start(), calls=%async_computation.4 | async-start | bytes 2949120 | tf_op jit(solution)/shard_map/all_gather | solution.py:186
  29.6 267.3 %reduce-scatter.2.cloned.1.call-start = ((), (), s32[]{:S(2)}) async-start(), calls=%async_computation.3 | async-start | bytes 2949120 | tf_op jit(solution)/shard_map/reduce_scatter | solution.py:221
  139.6 22.6 %copy-start.3 = (s32[3]{0:T(128)S(1)}, s32[3]{0:T(128)}, u32[]{:S(2)}) copy-start(s32[3]{0:T(128)} %param.19) | copy-start | bytes 40
  139.6 22.7 %copy-start.1 = (s32[3,14]{1,0:T(4,128)S(1)}, s32[3,14]{1,0:T(4,128)}, u32[]{:S(2)}) copy-start(s32[3,14]{1,0:T(4,128)} %param.18) | copy-start | bytes 508
  155.3 66.2 %collective-permute-start.3 = (bf16[2,3,128,768]{3,2,1,0:T(8,128)(2,1)}, bf16[2,3,128,768]{3,2,1,0:T(8,128)(2,1)}, u32[]{:S(2)}, u32[]{:S(2)}) collective-permute-start(bf16[2,3,128,768]{3,2,1,0:T(8,128)(2,1)} %bitcast.15), channel_id=1, source_target_pairs={{1,0},{2,1},{3,2},{5,4},{6,5},{7,6},{9,8},{10,9},{11,10},{13,12},{... | collective-permute-start | bytes 3538952 | tf_op jit(solution)/shard_map/ppermute | solution.py:200
  156.6 64.9 %collective-permute-start.2 = (bf16[2,3,128,768]{3,2,1,0:T(8,128)(2,1)}, bf16[2,3,128,768]{3,2,1,0:T(8,128)(2,1)}, u32[]{:S(2)}, u32[]{:S(2)}) collective-permute-start(bf16[2,3,128,768]{3,2,1,0:T(8,128)(2,1)} %bitcast.16), channel_id=1, source_target_pairs={{0,1},{1,2},{2,3},{4,5},{5,6},{6,7},{8,9},{9,10},{10,11},{12,13},{... | collective-permute-start | bytes 3538952 | tf_op jit(solution)/shard_map/ppermute | solution.py:199
  162.3 3.6 %collective-permute-start = (s32[3,15]{1,0:T(4,128)S(1)}, s32[3,15]{1,0:T(4,128)S(1)}, u32[]{:S(2)}, u32[]{:S(2)}) collective-permute-start(s32[3,15]{1,0:T(4,128)S(1)} %pad_add_fusion.1), channel_id=1, source_target_pairs={{0,16},{16,0},{1,17},{17,1},{2,18},{18,2},{3,19},{19,3},{4,20},{20... | collective-permute-start | bytes 548 | tf_op jit(solution)/shard_map/ppermute | solution.py:180
  240.2 9.2 %collective-permute-start.4 = (bf16[384,384]{1,0:T(8,128)(2,1)}, bf16[384,384]{1,0:T(8,128)(2,1)}, u32[]{:S(2)}, u32[]{:S(2)}) collective-permute-start(bf16[384,384]{1,0:T(8,128)(2,1)} %get-tuple-element.6), channel_id=1, source_target_pairs={{0,16},{16,0},{1,17},{17,1},{2,18},{18,2},{3,19},{19,3},{4,20},{20... | collective-permute-start | bytes 884744 | tf_op jit(solution)/shard_map/ppermute | solution.py:213
  255.6 41.4 %copy-start.2 = (f32[768]{0:T(1024)S(1)}, f32[768]{0:T(1024)}, u32[]{:S(2)}) copy-start(f32[768]{0:T(1024)} %param.15) | copy-start | bytes 9220
Sparse Core Ops, SparseCore 0:
  10.0 92.0 all-gather.6
  103.7 35.8 all-gather.4
  141.1 71.7 all-gather.8
  255.7 41.2 reduce-scatter.1

commit v2 on v1

--- a/solution.py
+++ b/solution.py
@@ -16,7 +16,7 @@
 
     @pl.when(part == 0)
     def _():
-        floats = x_ref[...].astype(F32)
+        floats = jnp.concatenate([x_ref[0, i] for i in range(x_ref.shape[1])], axis=1).astype(F32)
         center = jnp.mean(floats, axis=-1, keepdims=True)
         moved = floats - center
         spread = jnp.mean(moved * moved, axis=-1, keepdims=True)
@@ -48,31 +48,247 @@
             write(False)
 
 
-def project(x, scale, shift, w, gain, normalize):
-    rows, width = x.shape
+def project(x, scale, shift, w, first, gain, normalize):
+    slabs, pieces, rows, width = x.shape
+    width = pieces * width
     parts = len(normalize)
-    cols = w.shape[1] // parts
-    block = 256 if rows % 256 == 0 else rows
+    cols = w.shape[1] // 3
+    block = 192 if rows % 192 == 0 else rows
+    many = rows // block
     return pl.pallas_call(
         functools.partial(proj_kernel, normalize, gain.shape[0]),
-        grid=(rows // block, parts),
+        grid=(slabs * many, parts),
         in_specs=[
-            pl.BlockSpec((block, width), lambda i, j: (i, 0)),
+            pl.BlockSpec((1, pieces, block, width // pieces), lambda i, j: (i // many, 0, i % many, 0)),
             pl.BlockSpec((1, width), lambda i, j: (0, 0)),
             pl.BlockSpec((1, width), lambda i, j: (0, 0)),
-            pl.BlockSpec((width, cols), lambda i, j: (0, j)),
+            pl.BlockSpec((width, cols), lambda i, j: (0, j + first)),
             pl.BlockSpec((1, gain.shape[0]), lambda i, j: (0, 0)),
         ],
         out_specs=pl.BlockSpec((block, cols), lambda i, j: (i, j)),
-        out_shape=jax.ShapeDtypeStruct((rows, parts * cols), BF),
+        out_shape=jax.ShapeDtypeStruct((slabs * rows, parts * cols), BF),
         scratch_shapes=[pltpu.VMEM((block, width), BF)],
         cost_estimate=pl.CostEstimate(
-            flops=2 * rows * width * parts * cols,
-            bytes_accessed=2 * (rows * width + width * parts * cols + rows * parts * cols),
+            flops=2 * slabs * rows * width * parts * cols,
+            bytes_accessed=2 * (slabs * rows * width + width * parts * cols),
             transcendentals=0,
         ),
         name="project",
     )(x, scale.reshape(1, -1), shift.reshape(1, -1), w, gain.reshape(1, -1))
+
+
+def gather_kernel(tps, chunks, tok_in, w_in, tok, w_all, relay, transit, z_send, z_recv, p_send,
+                  p_recv, up_send, fwd_send, core_send, w_recv, t_recv, local):
+    s, t, b = lax.axis_index("slab"), lax.axis_index("tp"), lax.axis_index("band")
+    e, c = s % 2, t % 2
+    base = s - e
+    couples = tps // 2
+    couple = t // 2
+
+    def dev(slab, tp, band):
+        return {"slab": slab, "tp": tp, "band": band}
+
+    barrier = pltpu.get_barrier_semaphore()
+    peers = [dev(s, t, (b + i) % 4) for i in range(1, 4)]
+    for i in range(2):
+        for j in range(tps):
+            if i or j:
+                peers.append(dev(base + (e + i) % 2, (t + j) % tps, b))
+    for peer in peers:
+        pl.semaphore_signal(barrier, inc=1, device_id=peer, device_id_type=pl.DeviceIdType.MESH)
+    pl.semaphore_wait(barrier, len(peers))
+
+    def remote(src, dst, send, recv, peer):
+        return pltpu.make_async_remote_copy(
+            src, dst, send, recv, device_id=peer, device_id_type=pl.DeviceIdType.MESH
+        )
+
+    q_own = b % 2
+    planes = [b // 2, 2 + b // 2]
+    legs = [
+        remote(tok_in, relay.at[q_own], z_send.at[i], z_recv.at[q_own], dev(s, t, planes[i]))
+        for i in range(2)
+    ]
+    for i in range(2):
+
+        @pl.when(planes[i] != b)
+        def _(leg=legs[i]):
+            leg.start()
+
+    u = jnp.where(c == 1, b, 3 - b)
+    step = jnp.where(c == 1, 1, -1)
+    ahead, behind = jnp.clip(b + step, 0, 3), jnp.clip(b - step, 0, 3)
+
+    def slot(at):
+        return jnp.where(c == 1, at, 3 - at)
+
+    depth = w_in.shape[0] // chunks
+    rows = [pl.ds(k * depth, depth) for k in range(chunks)]
+    partner = dev(s, t + 1 - 2 * c, b)
+
+    def own(k, where):
+        if where == 0:
+            return remote(w_in.at[rows[k]], transit.at[rows[k]], up_send.at[k], t_recv.at[k], dev(s, t, ahead))
+        peer = dev(s, t, behind if where == 3 else ahead)
+        return remote(w_in.at[rows[k]], w_all.at[b, rows[k]], up_send.at[k], w_recv.at[b, k], peer)
+
+    def forward(src, k, at, n):
+        place = slot(at)
+        return remote(src, w_all.at[place, rows[k]], fwd_send.at[n, k], w_recv.at[place, k], dev(s, t, ahead))
+
+    def across(src, k, at):
+        place = slot(at)
+        return remote(src, w_all.at[place, rows[k]], core_send.at[at, k], w_recv.at[place, k], partner)
+
+    def arrived(k, at):
+        place = slot(at)
+        return remote(w_in.at[rows[k]], w_all.at[place, rows[k]], up_send.at[k], w_recv.at[place, k], partner)
+
+    keep = pltpu.make_async_copy(w_in, w_all.at[b], local.at[2])
+    for where in range(4):
+
+        @pl.when(u == where)
+        def _(where=where):
+            for k in range(chunks):
+                own(k, where).start()
+            if where >= 2:
+                keep.start()
+                for k in range(chunks):
+                    across(w_in.at[rows[k]], k, where).start()
+
+    def spread(src, q):
+        copies = []
+        for i in range(2):
+            for j in range(couples):
+                peer = dev(base + (e + i) % 2, 2 * ((couple + j) % couples) + q, b)
+                copies.append(remote(
+                    src, tok.at[e, t], p_send.at[q, i * couples + j], p_recv.at[e, t], peer
+                ))
+        return copies, pltpu.make_async_copy(src, tok.at[e, t], local.at[q])
+
+    for q in range(2):
+        source = 2 * (b % 2) + q
+
+        def send(src, q=q):
+            copies, here = spread(src, q)
+            for copy in copies[1:]:
+                copy.start()
+
+            @pl.when(c == q)
+            def _():
+                here.start()
+
+            @pl.when(c != q)
+            def _():
+                copies[0].start()
+
+        @pl.when(source == b)
+        def _(send=send):
+            send(tok_in)
+
+        @pl.when(source != b)
+        def _(send=send, q=q):
+            remote(tok_in, relay.at[q], z_send.at[0], z_recv.at[q], partner).wait_recv()
+            send(relay.at[q])
+
+    @pl.when(u == 1)
+    def _():
+        for k in range(chunks):
+            remote(w_in.at[rows[k]], transit.at[rows[k]], up_send.at[k], t_recv.at[k], partner).wait_recv()
+            forward(transit.at[rows[k]], k, 0, 0).start()
+
+    @pl.when(u == 2)
+    def _():
+        for n, at in enumerate((1, 0)):
+            for k in range(chunks):
+                arrived(k, at).wait_recv()
+                src = w_all.at[slot(at), rows[k]]
+                forward(src, k, at, n).start()
+                across(src, k, at).start()
+        for k in range(chunks):
+            arrived(k, 3).wait_recv()
+            across(w_all.at[slot(3), rows[k]], k, 3).start()
+
+    @pl.when(u == 3)
+    def _():
+        for at in (2, 1, 0):
+            for k in range(chunks):
+                arrived(k, at).wait_recv()
+                across(w_all.at[slot(at), rows[k]], k, at).start()
+
+    @pl.when(u < 2)
+    def _():
+        for at in range(4):
+            for k in range(chunks):
+                arrived(k, at).wait_recv()
+
+    for where in range(4):
+
+        @pl.when(u == where)
+        def _(where=where):
+            for k in range(chunks):
+                own(k, where).wait_send()
+                if where == 1:
+                    forward(transit.at[rows[k]], k, 0, 0).wait_send()
+                if where == 2:
+                    for n, at in enumerate((1, 0)):
+                        forward(w_all.at[slot(at), rows[k]], k, at, n).wait_send()
+                if where >= 2:
+                    for at in range(4):
+                        across(w_in.at[rows[k]], k, at).wait_send()
+            if where >= 2:
+                keep.wait()
+
+    for i in range(2):
+
+        @pl.when(planes[i] != b)
+        def _(leg=legs[i]):
+            leg.wait_send()
+
+    for q in range(2):
+        copies, here = spread(tok_in, q)
+        for copy in copies[1:]:
+            copy.wait_send()
+
+        @pl.when(c == q)
+        def _(here=here):
+            here.wait()
+
+        @pl.when(c != q)
+        def _(copy=copies[0]):
+            copy.wait_send()
+
+    for i in range(2):
+        for j in range(tps):
+            if i or j:
+                from_e, from_t = (e + i) % 2, (t + j) % tps
+                remote(
+                    tok_in, tok.at[from_e, from_t], p_send.at[0, 0], p_recv.at[from_e, from_t], partner
+                ).wait_recv()
+
+
+def gather_all(tokens, w, tps):
+    chunks = 2
+    dma = pltpu.SemaphoreType.DMA
+    vmem = pl.BlockSpec(memory_space=pltpu.VMEM)
+    return pl.pallas_call(
+        functools.partial(gather_kernel, tps, chunks),
+        out_shape=(
+            jax.ShapeDtypeStruct((2, tps) + tokens.shape, BF),
+            jax.ShapeDtypeStruct((4,) + w.shape, BF),
+        ),
+        in_specs=[vmem, vmem],
+        out_specs=(vmem, vmem),
+        scratch_shapes=[
+            pltpu.VMEM((2,) + tokens.shape, BF),
+            pltpu.VMEM(w.shape, BF),
+            dma((2,)), dma((2,)), dma((2, tps)), dma((2, tps)),
+            dma((chunks,)), dma((2, chunks)), dma((4, chunks)), dma((4, chunks)),
+            dma((chunks,)), dma((3,)),
+        ],
+        compiler_params=pltpu.CompilerParams(collective_id=0, has_side_effects=True),
+        name="gather_all",
+    )(tokens, w)
 
 
 def attend_kernel(head_size, place_ref, count_ref, q_ref, kv_ref, o_ref, sc):
@@ -172,51 +388,78 @@
     head_size = q_gain.shape[0]
     tiles = key_counts.shape[0]
     tile_len = tok_rows // tiles
+    tps = lax.axis_size("tp")
+    tp_pos = lax.axis_index("tp")
     swap = [(i, i ^ 1) for i in range(slabs)]
 
-    other = lax.ppermute(tokens, "slab", swap)
-    whole = lax.all_gather(jnp.concatenate([tokens, other], axis=0), "tp", axis=1, tiled=True)
-    lists = jnp.concatenate([tile_ids, key_counts[:, None]], axis=1)
-    lists = jnp.concatenate([lists, lax.ppermute(lists, "slab", swap)], axis=0)
-    ids, counts = lists[:, :-1], lists[:, -1]
+    band_here = 2 * (band_pos % 2) + tp_pos % 2
+
+    def flat(couple, core, side, low):
+        return (2 * couple + core) * bands + 2 * side + low
+
+    every = [
+        (couple, i // 4, i // 2 % 2, i % 2) for couple in range(tps // 2) for i in range(8)
+    ]
+    outward = [(flat(n, c, h, l), flat(n, h, l, c)) for n, c, h, l in every]
+    size = tps * bands
+    outward_swap = [
+        (i * size + source, (i ^ 1) * size + target)
+        for i in range(slabs)
+        for source, target in outward
+    ]
+    forward = [
+        (flat(n, i % 2, h, i // 2), flat(n, (i + 1) % 2, h, (i + 1) // 2))
+        for n in range(tps // 2)
+        for h in range(2)
+        for i in range(3)
+    ]
+
+    def both(ours, theirs, axis):
+        return jnp.where(
+            parity == 0,
+            jnp.concatenate([ours, theirs], axis=axis),
+            jnp.concatenate([theirs, ours], axis=axis),
+        )
 
     mine = lax.dynamic_slice_in_dim(w_qkv, parity * half, half, axis=2)
     depth = mine.shape[0]
-    w_kv = lax.all_gather(mine[:, 1:].reshape(depth, 2 * half), "band", axis=0, tiled=True)
-    w_q = lax.all_gather(mine[:, 0].reshape(depth, half), "band", axis=0, tiled=True)
-
-    joined = project(whole, scale, shift, w_kv, k_gain, (True, False))
+    whole, weights = gather_all(tokens, mine.reshape(depth, 3 * half), tps)
+    weights = weights.reshape(4 * depth, 3 * half)
+
+    lists = jnp.concatenate([tile_ids, key_counts[:, None]], axis=1)
+    ours = lax.ppermute(lists, ("tp", "band"), [(b, a) for a, b in outward])
+    theirs = lax.ppermute(
+        lists, ("slab", "tp", "band"), [(b, a) for a, b in outward_swap]
+    )
+    lists = both(ours, theirs, 0)
+    ids, counts = lists[:, :-1], lists[:, -1]
+
+    joined = project(whole, scale, shift, weights, 1, k_gain, (True, False))
     joined = joined.reshape(2, tiles, tile_len, 2 * half)
     if slabs > 2:
-        first = jnp.where(parity == 0, joined[0], joined[1])
-        second = jnp.where(parity == 0, joined[1], joined[0])
         up = [(i, i + 2) for i in range(slabs - 2)]
-        below = lax.ppermute(second, "slab", up)
-        above = lax.ppermute(first, "slab", [(b, a) for a, b in up])
+        below = lax.ppermute(joined[1], "slab", up)
+        above = lax.ppermute(joined[0], "slab", [(b, a) for a, b in up])
         joined = jnp.concatenate([joined, below[None], above[None]], axis=0)
     groups = joined.shape[0]
-    forward = [(i, i + 1) for i in range(bands - 1)]
-    left = lax.ppermute(joined, "band", forward)
-    right = lax.ppermute(joined, "band", [(b, a) for a, b in forward])
-    queries = project(whole, scale, shift, w_q, q_gain, (True,))
+    left = lax.ppermute(joined, ("tp", "band"), forward)
+    right = lax.ppermute(joined, ("tp", "band"), [(b, a) for a, b in forward])
+    queries = project(whole, scale, shift, weights, 0, q_gain, (True,))
     near = jnp.concatenate([left, joined, right], axis=0)
     near = near.reshape(3 * groups * tiles, tile_len, 2 * half)
 
     time_near = ids // (bands * tiles) - (slab_pos - parity)
-    group = jnp.where(
-        time_near < 0, 2, jnp.where(time_near > 1, 3, jnp.where(time_near == parity, 0, 1))
-    )
-    row_near = ids // tiles % bands - band_pos + 1
+    group = jnp.where(time_near < 0, 2, jnp.where(time_near > 1, 3, time_near))
+    row_near = ids // tiles % bands - band_here + 1
     place = (row_near * groups + group) * tiles + ids % tiles
 
     attended = attention(place, counts, queries, near, head_size)
-    back = lax.ppermute(attended[tok_rows:], "slab", swap)
-    ours = attended[:tok_rows]
-    joint = jnp.where(
-        parity == 0,
-        jnp.concatenate([ours, back], axis=1),
-        jnp.concatenate([back, ours], axis=1),
-    )
+    halves = attended.reshape(2, tok_rows, half)
+    ours = jnp.where(parity == 0, halves[0], halves[1])
+    theirs = jnp.where(parity == 0, halves[1], halves[0])
+    ours = lax.ppermute(ours, ("tp", "band"), outward)
+    theirs = lax.ppermute(theirs, ("slab", "tp", "band"), outward_swap)
+    joint = both(ours, theirs, 1)
     product = jnp.dot(joint, w_out, preferred_element_type=F32)
     shares = lax.psum_scatter(
         product.astype(BF), "tp", scatter_dimension=1, tiled=True

time: 307 us -> 235 us (0.77)
  waiting for transfers between devices: 220 us -> 56.8 us
  Pallas kernels: 37.6 us -> 130 us
  local copies, waits for them, and re-layouts: 6.94 us -> 11.9 us
  starting transfers between devices: 13.1 us -> 8.76 us
    all_gather x3 -> x0, waiting for transfers between devices: 155 us -> none  [the longest x1 72.4 us: shards(): lax.all_gather(mine[:, 1:].reshape(depth, 2 * half), 'band', axis=0, tile...]
    pallas_call x0 -> x1, Pallas kernels: none -> 90.8 us  [gather_all(): pl.pallas_call(functools.partial(gather_kernel, tps, chunks), out_shape=(...]
    ppermute x5 -> x6, waiting for transfers between devices: 23.2 us -> 5.27 us  [the longest x1 5.26 us: shards(): theirs = lax.ppermute(theirs, ('slab', 'tp', 'band'), outward_swap)]
    reduce_scatter x1, waiting for transfers between devices: 41.4 us -> 51.6 us  [shards(): lax.psum_scatter(product.astype(BF), 'tp', scatter_dimension=1, tiled=True)]
    ppermute x5 -> x6, starting transfers between devices: 13 us -> 8.76 us  [the longest x1 4.07 us: shards(): left = lax.ppermute(joined, ('tp', 'band'), forward)]
    unnamed x9, local copies, waits for them, and re-layouts: 2.13 us -> 5.87 us
  transfers between devices with their start and end apart: 9 -> 7, of which waited for: 7 -> 2; matrix products, arithmetic and copies ran while one was open for 2% -> 1% of each run, Pallas kernels for 8% -> 4%
where the time goes in v2:
time: 235 us; the launch traced here: 234 us
  Pallas kernels  130 us (55%)
  waiting for transfers between devices  56.8 us (24%)
  between operations  13.5 us (6%)
  local copies, waits for them, and re-layouts  11.9 us (5%)
  starting transfers between devices  8.76 us (4%)
  other arithmetic  7.17 us (3%)
  matrix products  5.77 us (2%)
    pallas_call x1, Pallas kernels, gather_all(): pl.pallas_call(functools.partial(gather_kernel, tps, chunks), out_shape=(...  90.8 us
    reduce_scatter x1, waiting for transfers between devices, shards(): lax.psum_scatter(product.astype(BF), 'tp', scatter_dimension=1, tiled=True)  51.6 us
    pallas_call x2, Pallas kernels, project(): pl.pallas_call(functools.partial(proj_kernel, normalize, gain.shape[0]),...  26.1 us
    pallas_call x1, Pallas kernels, attention(): pl.pallas_call(functools.partial(attend_kernel, head_size), grid_spec=plt...  13.4 us
    unnamed x9, local copies, waits for them, and re-layouts  5.87 us
    dot_general x1, matrix products, shards(): product = jnp.dot(joint, w_out, preferred_element_type=F32)  5.77 us
    ppermute x1, waiting for transfers between devices, shards(): theirs = lax.ppermute(theirs, ('slab', 'tp', 'band'), outward_swap)  5.26 us
  transfers between devices with their start and end apart: 7, of which 2 were waited for; matrix products, arithmetic and copies ran while one was open for 1% of the time, Pallas kernels for 4%

profile of v2, /device:TPU:0, one launch (start us, length us, event | category | flops | bytes accessed | tf_op | source)
XLA Modules:
  0.0 234.2 jit_solution(2666673816644220027)
XLA Ops:
  6.5 0.0 copy-start
  6.5 0.0 reduce-scatter.2.cloned.1.call-start
  6.5 2.0 copy-done
  8.5 1.4 constant_dynamic-slice_fusion
  9.9 3.9 %copy.16 = bf16[768,3,384]{0,2,1:T(8,128)(2,1)} copy(bf16[768,3,384]{2,0,1:T(8,128)(2,1)} %constant_dynamic-slice_fusion) | data formatting | bytes 3538944
  13.8 3.9 %copy.15.w_in = bf16[768,1152]{1,0:T(8,128)(2,1)} copy(bf16[768,1152]{0,1:T(8,128)(2,1)} %bitcast.10) | data formatting | bytes 3538944 | tf_op jit(solution)/shard_map/reshape | solution.py:426
  17.6 90.8 %gather_all.1 = (bf16[2,4,384,768]{3,2,1,0:T(8,128)(2,1)}, bf16[4,768,1152]{2,1,0:T(8,128)(2,1)}) custom-call(bf16[384,768]{1,0:T(8,128)(2,1)} %tok_in.1, bf16[768,1152]{1,0:T(8,128)(2,1)} %copy.15.w_in), custom_call_target="tpu_custom_call" | custom-call | tf_op jit(solution)/shard_map/gather_all/pallas_call | solution.py:274
  108.4 0.0 copy-start.3
  108.4 0.0 copy-start.2
  108.5 17.2 %project.3 = bf16[768,768]{1,0:T(8,128)(2,1)} custom-call(bf16[2,4,384,768]{3,2,1,0:T(8,128)(2,1)} %get-tuple-element.7.x_ref, f32[1,3072]{1,0:T(1,128)} %bitcast.17, f32[1,3072]{1,0:T(1,128)} %bitcast.19, bf16[3072,1152]{1,0:T(8,128)(2,1)} %bitcast.11, f32[1,128]{1,0:T(1,128)} %bitcast.23), custom_call_target="tpu_custom_call" | custom-call | flops 3623878656 | bytes 9437184 | tf_op jit(solution)/shard_map/project/pallas_call | solution.py:58
  125.7 1.3 collective-permute-start.3
  127.0 4.1 %collective-permute-start.2 = (bf16[2,3,128,768]{3,2,1,0:T(8,128)(2,1)}, bf16[2,3,128,768]{3,2,1,0:T(8,128)(2,1)}, u32[]{:S(2)}, u32[]{:S(2)}) collective-permute-start(bf16[2,3,128,768]{3,2,1,0:T(8,128)(2,1)} %bitcast.15), channel_id=1, source_target_pairs={{0,4},{4,1},{1,5},{2,6},{6,3},{3,7},{8,12},{12,9},{9,13},{10,14},{... | collective-permute-start | bytes 3538952 | tf_op jit(solution)/shard_map/ppermute | solution.py:445
  131.0 0.0 copy-done.3
  131.0 0.1 copy.13
  131.1 0.0 copy-done.2
  131.1 0.1 pad_add_fusion
  131.2 0.6 collective-permute-start.1
  131.8 0.6 collective-permute-start
  132.4 8.9 %project.2.q_ref = bf16[768,384]{1,0:T(8,128)(2,1)} custom-call(bf16[2,4,384,768]{3,2,1,0:T(8,128)(2,1)} %get-tuple-element.7.x_ref, f32[1,3072]{1,0:T(1,128)} %bitcast.18, f32[1,3072]{1,0:T(1,128)} %bitcast.20, bf16[3072,1152]{1,0:T(8,128)(2,1)} %bitcast.12, f32[1,128]{1,0:T(1,128)} %bitcast.21), custom_call_target="tpu_custom_call" | custom-call | flops 1811939328 | bytes 7077888 | tf_op jit(solution)/shard_map/project/pallas_call | solution.py:58
  141.3 0.0 collective-permute-done.1
  141.3 0.0 collective-permute-done
  141.4 0.7 slice_reduce_fusion.count_ref
  142.1 0.6 fusion.12.place_ref
  142.7 0.0 collective-permute-done.3
  142.7 0.0 collective-permute-done.2
  142.7 3.4 %pad_maximum_fusion = bf16[6,3,128,768]{3,2,1,0:T(8,128)(2,1)} fusion(bf16[2,3,128,768]{3,2,1,0:T(8,128)(2,1)} %collective-permute-done.3, bf16[2,3,128,768]{3,2,1,0:T(8,128)(2,1)} %bitcast.16, bf16[2,3,128,768]{3,2,1,0:T(8,128)(2,1)} %collective-permute-done.2), kind=kLoop, calls=%fused_computation.1 | loop fusion | flops 3538944 | bytes 7077888 | tf_op jit(solution)/shard_map/concatenate | solution.py:448
  146.1 13.4 %attend.1 = bf16[768,384]{1,0:T(8,128)(2,1)} custom-call(s32[6,14]{1,0:T(8,128)} %fusion.12.place_ref, s32[6]{0:T(128)} %slice_reduce_fusion.count_ref, bf16[768,384]{1,0:T(8,128)(2,1)} %project.2.q_ref, bf16[18,128,768]{2,1,0:T(8,128)(2,1)} %bitcast.13), custom_call_target="tpu_custom_call" | custom-call | flops 2113929216 | bytes 4718592 | tf_op jit(solution)/shard_map/attend/pallas_call | solution.py:359
  159.4 1.1 broadcast_select_fusion.1
  160.6 0.7 collective-permute-start.4
  161.2 1.5 collective-permute-start.5
  162.8 0.0 collective-permute-done.4
  162.8 5.3 %collective-permute-done.5 = bf16[384,384]{1,0:T(8,128)(2,1)S(1)} collective-permute-done((bf16[384,384]{1,0:T(8,128)(2,1)S(1)}, bf16[384,384]{1,0:T(8,128)(2,1)S(1)}, u32[]{:S(2)}, u32[]{:S(2)}) %collective-permute-start.5) | collective-permute-done | bytes 294944 | tf_op jit(solution)/shard_map/ppermute | solution.py:461
  168.0 5.8 %convolution_convert_fusion = bf16[384,3072]{1,0:T(8,128)(2,1)} fusion(bf16[768,3072]{1,0:T(8,128)(2,1)} %param.12, bf16[384,384]{1,0:T(8,128)(2,1)S(1)} %collective-permute-done.5, bf16[384,384]{1,0:T(8,128)(2,1)S(1)} %collective-permute-done.4, pred[]{:T(512)S(6)} %eq.13), kind=kOutput, calls=%fused_computation | convolution fusion | flops 1815773184 | bytes 7667713 | tf_op jit(solution)/shard_map/dot_general | solution.py:463
  173.8 0.0 copy-start.1
  173.8 0.0 reduce-scatter.2.cloned.1.call-update
  173.8 51.6 %reduce-scatter.2.cloned.1.call-done = bf16[384,768]{1,0:T(8,128)(2,1)} async-done(((bf16[384,3072]{1,0:T(8,128)(2,1)}), bf16[384,768]{1,0:T(8,128)(2,1)}) %reduce-scatter.2.cloned.1.call-update) | async-done | bytes 589840 | tf_op jit(solution)/shard_map/reduce_scatter | solution.py:464
  225.4 0.0 copy-done.1
  225.4 2.0 multiply_convert_fusion
  (1 shorter events, 0.0 us)
Async XLA Ops:
  6.5 2.0 copy-start
  6.5 218.8 %reduce-scatter.2.cloned.1.call-start = ((), (), s32[]{:S(2)}) async-start(), calls=%async_computation.1 | async-start | bytes 2949120 | tf_op jit(solution)/shard_map/reduce_scatter | solution.py:464
  108.4 22.6 %copy-start.3 = (s32[3]{0:T(128)S(1)}, s32[3]{0:T(128)}, u32[]{:S(2)}) copy-start(s32[3]{0:T(128)} %param.19) | copy-start | bytes 40
  108.4 22.7 %copy-start.2 = (s32[3,14]{1,0:T(4,128)S(1)}, s32[3,14]{1,0:T(4,128)}, u32[]{:S(2)}) copy-start(s32[3,14]{1,0:T(4,128)} %param.18) | copy-start | bytes 508
  125.7 17.0 %collective-permute-start.3 = (bf16[2,3,128,768]{3,2,1,0:T(8,128)(2,1)}, bf16[2,3,128,768]{3,2,1,0:T(8,128)(2,1)}, u32[]{:S(2)}, u32[]{:S(2)}) collective-permute-start(bf16[2,3,128,768]{3,2,1,0:T(8,128)(2,1)} %bitcast.14), channel_id=1, source_target_pairs={{4,0},{1,4},{5,1},{6,2},{3,6},{7,3},{12,8},{9,12},{13,9},{14,10},{... | collective-permute-start | bytes 3538952 | tf_op jit(solution)/shard_map/ppermute | solution.py:446
  127.0 15.7 %collective-permute-start.2 = (bf16[2,3,128,768]{3,2,1,0:T(8,128)(2,1)}, bf16[2,3,128,768]{3,2,1,0:T(8,128)(2,1)}, u32[]{:S(2)}, u32[]{:S(2)}) collective-permute-start(bf16[2,3,128,768]{3,2,1,0:T(8,128)(2,1)} %bitcast.15), channel_id=1, source_target_pairs={{0,4},{4,1},{1,5},{2,6},{6,3},{3,7},{8,12},{12,9},{9,13},{10,14},{... | collective-permute-start | bytes 3538952 | tf_op jit(solution)/shard_map/ppermute | solution.py:445
  131.2 10.1 %collective-permute-start.1 = (s32[3,15]{1,0:T(4,128)S(1)}, s32[3,15]{1,0:T(4,128)S(1)}, u32[]{:S(2)}, u32[]{:S(2)}) collective-permute-start(s32[3,15]{1,0:T(4,128)S(1)} %pad_add_fusion), channel_id=1, source_target_pairs={{16,0},{18,1},{20,2},{22,3},{17,4},{19,5},{21,6},{23,7},{24,8},{26... | collective-permute-start | bytes 548 | tf_op jit(solution)/shard_map/ppermute | solution.py:431
  131.8 9.6 %collective-permute-start = (s32[3,15]{1,0:T(4,128)S(1)}, s32[3,15]{1,0:T(4,128)S(1)}, u32[]{:S(2)}, u32[]{:S(2)}) collective-permute-start(s32[3,15]{1,0:T(4,128)S(1)} %pad_add_fusion), channel_id=1, source_target_pairs={{0,0},{2,1},{4,2},{6,3},{1,4},{3,5},{5,6},{7,7},{8,8},{10,9},{12,1... | collective-permute-start | bytes 548 | tf_op jit(solution)/shard_map/ppermute | solution.py:430
  160.6 2.2 collective-permute-start.4
  161.2 6.8 %collective-permute-start.5 = (bf16[384,384]{1,0:T(8,128)(2,1)S(1)}, bf16[384,384]{1,0:T(8,128)(2,1)S(1)}, u32[]{:S(2)}, u32[]{:S(2)}) collective-permute-start(bf16[384,384]{1,0:T(8,128)(2,1)S(1)} %get-tuple-element.10), channel_id=1, source_target_pairs={{0,16},{1,18},{2,20},{3,22},{4,17},{5,19},{6,21},{7,23},{8,24},{9,... | collective-permute-start | bytes 884744 | tf_op jit(solution)/shard_map/ppermute | solution.py:461
  173.8 51.6 %copy-start.1 = (f32[768]{0:T(1024)S(1)}, f32[768]{0:T(1024)}, u32[]{:S(2)}) copy-start(f32[768]{0:T(1024)} %param.15) | copy-start | bytes 9220
Sparse Core Ops, SparseCore 0:
  173.9 51.3 reduce-scatter.1

commit v3 on v2

--- a/solution.py
+++ b/solution.py
@@ -24,7 +24,8 @@
             moved * lax.rsqrt(spread + 1e-06) * (1.0 + scale_ref[...]) + shift_ref[...]
         ).astype(BF)
 
-    product = jnp.dot(normed[...], w_ref[...], preferred_element_type=F32)
+    weights = w_ref[...].reshape(normed.shape[1], w_ref.shape[3])
+    product = jnp.dot(normed[...], weights, preferred_element_type=F32)
 
     def write(normed_part):
         for head in range(product.shape[1] // head_size):
@@ -52,7 +53,7 @@
     slabs, pieces, rows, width = x.shape
     width = pieces * width
     parts = len(normalize)
-    cols = w.shape[1] // 3
+    cols = w.shape[3]
     block = 192 if rows % 192 == 0 else rows
     many = rows // block
     return pl.pallas_call(
@@ -62,7 +63,7 @@
             pl.BlockSpec((1, pieces, block, width // pieces), lambda i, j: (i // many, 0, i % many, 0)),
             pl.BlockSpec((1, width), lambda i, j: (0, 0)),
             pl.BlockSpec((1, width), lambda i, j: (0, 0)),
-            pl.BlockSpec((width, cols), lambda i, j: (0, j + first)),
+            pl.BlockSpec((w.shape[0], 1) + w.shape[2:], lambda i, j: (0, j + first, 0, 0)),
             pl.BlockSpec((1, gain.shape[0]), lambda i, j: (0, 0)),
         ],
         out_specs=pl.BlockSpec((block, cols), lambda i, j: (i, j)),
@@ -122,8 +123,7 @@
     def slot(at):
         return jnp.where(c == 1, at, 3 - at)
 
-    depth = w_in.shape[0] // chunks
-    rows = [pl.ds(k * depth, depth) for k in range(chunks)]
+    rows = list(range(chunks))
     partner = dev(s, t + 1 - 2 * c, b)
 
     def own(k, where):
@@ -268,7 +268,7 @@
 
 
 def gather_all(tokens, w, tps):
-    chunks = 2
+    chunks = w.shape[0]
     dma = pltpu.SemaphoreType.DMA
     vmem = pl.BlockSpec(memory_space=pltpu.VMEM)
     return pl.pallas_call(
@@ -291,8 +291,16 @@
     )(tokens, w)
 
 
-def attend_kernel(head_size, place_ref, count_ref, q_ref, kv_ref, o_ref, sc):
+def attend_kernel(head_size, place_ref, count_ref, q_ref, a_ref, b_ref, c_ref, o_ref, sc, kv_ref):
     tile = pl.program_id(0)
+
+    @pl.when(tile == 0)
+    def _():
+        many = a_ref.shape[0]
+        for n, ref in enumerate((a_ref, b_ref, c_ref)):
+            for i in range(many):
+                kv_ref[n * many + i] = ref[i]
+
     tile_len, feats = q_ref.shape
     heads = feats // head_size
     count = count_ref[tile]
@@ -353,7 +361,7 @@
     rows, feats = queries.shape
     tile_len = rows // tiles
     heads = feats // head_size
-    many = keys_values.shape[0]
+    many = keys_values[0].shape[0]
     if slots % 2:
         place = jnp.pad(place, ((0, 0), (0, 1)))
     return pl.pallas_call(
@@ -363,10 +371,12 @@
             grid=(tiles,),
             in_specs=[
                 pl.BlockSpec((tile_len, feats), lambda i, a, b: (i, 0)),
-                pl.BlockSpec((many, tile_len, 2 * feats), lambda i, a, b: (0, 0, 0)),
+            ] + [pl.BlockSpec((many, tile_len, 2 * feats), lambda i, a, b: (0, 0, 0))] * 3,
+            out_specs=pl.BlockSpec((tile_len, feats), lambda i, a, b: (i, 0)),
+            scratch_shapes=[
+                pltpu.VMEM(((slots + 1) // 2, heads, tile_len, 2 * tile_len), F32),
+                pltpu.VMEM((3 * many, tile_len, 2 * feats), BF),
             ],
-            out_specs=pl.BlockSpec((tile_len, feats), lambda i, a, b: (i, 0)),
-            scratch_shapes=[pltpu.VMEM(((slots + 1) // 2, heads, tile_len, 2 * tile_len), F32)],
         ),
         out_shape=jax.ShapeDtypeStruct((rows, feats), BF),
         cost_estimate=pl.CostEstimate(
@@ -375,7 +385,121 @@
             transcendentals=rows * slots * tile_len * heads,
         ),
         name="attend",
-    )(place, counts, queries, keys_values)
+    )(place, counts, queries, *keys_values)
+
+
+def finish_kernel(tps, att, w_out, gate, out, joint, core_out, core_in, far_out, far_in, j_send,
+                  j_recv, c_send, c_recv, f_send, f_recv, local):
+    s, t, b = lax.axis_index("slab"), lax.axis_index("tp"), lax.axis_index("band")
+    e, c = s % 2, t % 2
+    couples, couple = tps // 2, t // 2
+    half = att.shape[2]
+    width = out.shape[1]
+    other = s + 1 - 2 * e
+    alone = (c == b // 2) & (c == b % 2)
+    kind = pl.DeviceIdType.MESH
+
+    def dev(slab, tp, band):
+        return {"slab": slab, "tp": tp, "band": band}
+
+    to_t, to_b = 2 * couple + b // 2, 2 * (b % 2) + c
+    from_t, from_b = 2 * couple + b % 2, 2 * c + b // 2
+    partner = dev(s, t + 1 - 2 * c, b)
+    across = [dev(s, 2 * ((couple + j) % couples) + c, b) for j in range(1, couples)]
+    barrier = pltpu.get_barrier_semaphore()
+    peers = [dev(other, to_t, to_b), dev(other, from_t, from_b), partner] + across
+    for peer in peers:
+        pl.semaphore_signal(barrier, inc=1, device_id=peer, device_id_type=kind)
+
+    @pl.when(jnp.logical_not(alone))
+    def _():
+        for peer in (dev(s, to_t, to_b), dev(s, from_t, from_b)):
+            pl.semaphore_signal(barrier, inc=1, device_id=peer, device_id_type=kind)
+
+    pl.semaphore_wait(barrier, len(peers) + jnp.where(alone, 0, 2))
+
+    def remote(src, dst, send, recv, peer):
+        return pltpu.make_async_remote_copy(src, dst, send, recv, device_id=peer, device_id_type=kind)
+
+    away = remote(att.at[1 - e], joint.at[e], j_send.at[1], j_recv.at[e], dev(other, to_t, to_b))
+    home = remote(att.at[e], joint.at[e], j_send.at[0], j_recv.at[e], dev(s, to_t, to_b))
+    here = pltpu.make_async_copy(att.at[e], joint.at[e], local.at[0])
+    away.start()
+
+    @pl.when(alone)
+    def _():
+        here.start()
+        here.wait()
+
+    @pl.when(jnp.logical_not(alone))
+    def _():
+        home.start()
+        home.wait_send()
+        home.wait_recv()
+
+    away.wait_send()
+    remote(att.at[e], joint.at[1 - e], j_send.at[1], j_recv.at[1 - e], partner).wait_recv()
+
+    def share(j, core):
+        target = 2 * ((couple + j) % couples) + core
+        cols = pl.ds(pl.multiple_of(target * width, width), width)
+        total = jnp.dot(joint[0], w_out[:half, cols], preferred_element_type=F32)
+        return total + jnp.dot(joint[1], w_out[half:, cols], preferred_element_type=F32)
+
+    order = list(range(1, couples)) + [0]
+    swaps = [
+        remote(core_out.at[j], core_in.at[j], c_send.at[j], c_recv.at[j], partner)
+        for j in range(couples)
+    ]
+    sends = [
+        remote(far_out.at[j - 1], far_in.at[j - 1], f_send.at[j - 1], f_recv.at[j - 1], across[j - 1])
+        for j in range(1, couples)
+    ]
+    for j in order[:-1]:
+        core_out[j] = share(j, 1 - c)
+        swaps[j].start()
+        mine = share(j, c)
+        swaps[j].wait_recv()
+        far_out[j - 1] = (mine + core_in[j]).astype(BF)
+        sends[j - 1].start()
+    core_out[0] = share(0, 1 - c)
+    swaps[0].start()
+    total = share(0, c)
+    swaps[0].wait_recv()
+    core_in[0] = total + core_in[0]
+    for j in range(1, couples):
+        sends[j - 1].wait_recv()
+        core_in[0] += far_in[j - 1].astype(F32)
+    out[...] = (gate[...] * core_in[0]).astype(BF)
+    for j in range(1, couples):
+        sends[j - 1].wait_send()
+    for j in range(couples):
+        swaps[j].wait_send()
+
+
+def finish(att, w_out, gate, tps):
+    rows, half = att.shape[1:]
+    width = gate.shape[0]
+    couples = tps // 2
+    dma = pltpu.SemaphoreType.DMA
+    vmem = pl.BlockSpec(memory_space=pltpu.VMEM)
+    return pl.pallas_call(
+        functools.partial(finish_kernel, tps),
+        out_shape=jax.ShapeDtypeStruct((rows, width), BF),
+        in_specs=[vmem] * 3,
+        out_specs=vmem,
+        scratch_shapes=[
+            pltpu.VMEM((2, rows, half), BF),
+            pltpu.VMEM((couples, rows, width), F32),
+            pltpu.VMEM((couples, rows, width), F32),
+            pltpu.VMEM((couples - 1, rows, width), BF),
+            pltpu.VMEM((couples - 1, rows, width), BF),
+            dma((2,)), dma((2,)), dma((couples,)), dma((couples,)),
+            dma((couples - 1,)), dma((couples - 1,)), dma((1,)),
+        ],
+        compiler_params=pltpu.CompilerParams(collective_id=1, has_side_effects=True),
+        name="finish",
+    )(att, w_out, gate.reshape(1, -1))
 
 
 def shards(tokens, w_qkv, w_out, shift, scale, gate, q_gain, k_gain, tile_ids, key_counts):
@@ -422,9 +546,7 @@
         )
 
     mine = lax.dynamic_slice_in_dim(w_qkv, parity * half, half, axis=2)
-    depth = mine.shape[0]
-    whole, weights = gather_all(tokens, mine.reshape(depth, 3 * half), tps)
-    weights = weights.reshape(4 * depth, 3 * half)
+    whole, weights = gather_all(tokens, jnp.stack([mine[:, i] for i in range(3)]), tps)
 
     lists = jnp.concatenate([tile_ids, key_counts[:, None]], axis=1)
     ours = lax.ppermute(lists, ("tp", "band"), [(b, a) for a, b in outward])
@@ -445,8 +567,7 @@
     left = lax.ppermute(joined, ("tp", "band"), forward)
     right = lax.ppermute(joined, ("tp", "band"), [(b, a) for a, b in forward])
     queries = project(whole, scale, shift, weights, 0, q_gain, (True,))
-    near = jnp.concatenate([left, joined, right], axis=0)
-    near = near.reshape(3 * groups * tiles, tile_len, 2 * half)
+    near = [part.reshape(groups * tiles, tile_len, 2 * half) for part in (left, joined, right)]
 
     time_near = ids // (bands * tiles) - (slab_pos - parity)
     group = jnp.where(time_near < 0, 2, jnp.where(time_near > 1, 3, time_near))
@@ -454,17 +575,7 @@
     place = (row_near * groups + group) * tiles + ids % tiles
 
     attended = attention(place, counts, queries, near, head_size)
-    halves = attended.reshape(2, tok_rows, half)
-    ours = jnp.where(parity == 0, halves[0], halves[1])
-    theirs = jnp.where(parity == 0, halves[1], halves[0])
-    ours = lax.ppermute(ours, ("tp", "band"), outward)
-    theirs = lax.ppermute(theirs, ("slab", "tp", "band"), outward_swap)
-    joint = both(ours, theirs, 1)
-    product = jnp.dot(joint, w_out, preferred_element_type=F32)
-    shares = lax.psum_scatter(
-        product.astype(BF), "tp", scatter_dimension=1, tiled=True
-    ).astype(F32)
-    return (gate * shares).astype(BF)
+    return finish(attended.reshape(2, tok_rows, half), w_out, gate, tps)
 
 
 def solution(mesh):

time: 235 us -> 190 us (0.81)
  waiting for transfers between devices: 56.8 us -> 0.01 us
  Pallas kernels: 130 us -> 177 us
  between operations: 13.5 us -> 0.13 us
  matrix products: 5.77 us -> 0 us
  local copies, waits for them, and re-layouts: 11.9 us -> 6.4 us
  other arithmetic: 7.17 us -> 2.24 us
  starting transfers between devices: 8.76 us -> 4.84 us
    reduce_scatter x1 -> x0, waiting for transfers between devices: 51.6 us -> none  [shards(): lax.psum_scatter(product.astype(BF), 'tp', scatter_dimension=1, tiled=True)]
    pallas_call x0 -> x1, Pallas kernels: none -> 47.5 us  [finish(): pl.pallas_call(functools.partial(finish_kernel, tps), out_shape=jax.Shape...]
    dot_general x1 -> x0, matrix products: 5.77 us -> none  [shards(): product = jnp.dot(joint, w_out, preferred_element_type=F32)]
    ppermute x2 -> x0, waiting for transfers between devices: 5.26 us -> none  [the longest x1 5.26 us: shards(): theirs = lax.ppermute(theirs, ('slab', 'tp', 'band'), outward_swap)]
    pallas_call x1, Pallas kernels: 90.8 us -> 87.3 us  [gather_all(): pl.pallas_call(functools.partial(gather_kernel, tps, chunks), out_shape=(...]
    concatenate x1 -> x0, other arithmetic: 3.39 us -> none  [shards(): near = jnp.concatenate([left, joined, right], axis=0)]
    reshape x1, local copies, waits for them, and re-layouts: 3.88 us -> 0.6 us  [finish(): gate.reshape(1, -1)]
    pallas_call x1, Pallas kernels: 13.4 us -> 16.5 us  [attention(): pl.pallas_call(functools.partial(attend_kernel, head_size), grid_spec=plt...]
  transfers between devices with their start and end apart: 7 -> 4, of which waited for: 2 -> 0; matrix products, arithmetic and copies ran while one was open for 1% -> 1% of each run, Pallas kernels for 4% -> 5%
where the time goes in v3:
time: 190 us; the launch traced here: 191 us
  Pallas kernels  177 us (93%)
  local copies, waits for them, and re-layouts  6.4 us (3%)
  starting transfers between devices  4.84 us (3%)
  other arithmetic  2.24 us (1%)
    pallas_call x1, Pallas kernels, gather_all(): pl.pallas_call(functools.partial(gather_kernel, tps, chunks), out_shape=(...  87.3 us
    pallas_call x1, Pallas kernels, finish(): pl.pallas_call(functools.partial(finish_kernel, tps), out_shape=jax.Shape...  47.5 us
    pallas_call x2, Pallas kernels, project(): pl.pallas_call(functools.partial(proj_kernel, normalize, gain.shape[0]),...  26.1 us
    pallas_call x1, Pallas kernels, attention(): pl.pallas_call(functools.partial(attend_kernel, head_size), grid_spec=plt...  16.5 us
  transfers between devices with their start and end apart: 4, of which 0 were waited for; matrix products, arithmetic and copies ran while one was open for 1% of the time, Pallas kernels for 5%

profile of v3, /device:TPU:0, one launch (start us, length us, event | category | flops | bytes accessed | tf_op | source)
XLA Modules:
  0.0 191.0 jit_solution(276346512822767758)
XLA Ops:
  0.0 1.6 dynamic-slice_bitcast_fusion.2
  1.6 1.5 pad_maximum_fusion.w_in
  3.1 87.3 %gather_all.1 = (bf16[2,4,384,768]{3,2,1,0:T(8,128)(2,1)}, bf16[4,3,768,384]{3,2,1,0:T(8,128)(2,1)}) custom-call(bf16[384,768]{1,0:T(8,128)(2,1)} %tok_in.1, bf16[3,768,384]{2,1,0:T(8,128)(2,1)} %pad_maximum_fusion.w_in), custom_call_target="tpu_custom_call" | custom-call | tf_op jit(solution)/shard_map/gather_all/pallas_call | solution.py:274
  90.4 0.0 copy-start.2
  90.5 0.0 copy-start.1
  90.5 0.0 copy-start
  90.5 17.2 %project.3 = bf16[768,768]{1,0:T(8,128)(2,1)} custom-call(bf16[2,4,384,768]{3,2,1,0:T(8,128)(2,1)} %get-tuple-element.7.x_ref, f32[1,3072]{1,0:T(1,128)} %bitcast.17, f32[1,3072]{1,0:T(1,128)} %bitcast.19, bf16[4,3,768,384]{3,2,1,0:T(8,128)(2,1)} %get-tuple-element.8.w_ref, f32[1,128]{1,0:T(1,128)} %bitcast.28), custom_call_target="tpu_custom_call" | custom-call | flops 3623878656 | bytes 9437184 | tf_op jit(solution)/shard_map/project/pallas_call | solution.py:59
  107.7 2.3 %collective-permute-start.2 = (bf16[2,3,128,768]{3,2,1,0:T(8,128)(2,1)}, bf16[2,3,128,768]{3,2,1,0:T(8,128)(2,1)S(1)}, u32[]{:S(2)}, u32[]{:S(2)}) collective-permute-start(bf16[2,3,128,768]{3,2,1,0:T(8,128)(2,1)} %bitcast.23), channel_id=1, source_target_pairs={{0,4},{4,1},{1,5},{2,6},{6,3},{3,7},{8,12},{12,9},{9,13},{10,14},{... | collective-permute-start | bytes 3538952 | tf_op jit(solution)/shard_map/ppermute | solution.py:567
  110.1 1.3 collective-permute-start.3
  111.4 0.0 copy-done.2
  111.4 0.1 copy.12
  111.5 0.0 copy-done.1
  111.5 0.1 pad_add_fusion
  111.6 0.6 collective-permute-start.1
  112.1 0.6 collective-permute-start
  112.8 0.0 copy-done
  112.8 0.6 reshape.37.gate
  113.4 8.9 %project.2.q_ref = bf16[768,384]{1,0:T(8,128)(2,1)} custom-call(bf16[2,4,384,768]{3,2,1,0:T(8,128)(2,1)} %get-tuple-element.7.x_ref, f32[1,3072]{1,0:T(1,128)} %bitcast.18, f32[1,3072]{1,0:T(1,128)} %bitcast.20, bf16[4,3,768,384]{3,2,1,0:T(8,128)(2,1)} %get-tuple-element.8.w_ref, f32[1,128]{1,0:T(1,128)} %bitcast.21), custom_call_target="tpu_custom_call" | custom-call | flops 1811939328 | bytes 7077888 | tf_op jit(solution)/shard_map/project/pallas_call | solution.py:59
  122.3 0.0 collective-permute-done.1
  122.3 0.0 collective-permute-done
  122.3 0.8 slice_reduce_fusion.count_ref
  123.1 0.6 fusion.6.place_ref
  123.7 0.0 collective-permute-done.2
  123.7 0.0 copy-start.3
  123.7 0.0 collective-permute-done.3
  123.7 0.0 copy-start.4
  123.7 1.0 copy-done.3
  124.7 0.4 copy-done.4
  125.1 16.5 %attend.1 = bf16[768,384]{1,0:T(8,128)(2,1)} custom-call(s32[6,14]{1,0:T(8,128)} %fusion.6.place_ref, s32[6]{0:T(128)} %slice_reduce_fusion.count_ref, bf16[768,384]{1,0:T(8,128)(2,1)} %project.2.q_ref, bf16[6,128,768]{2,1,0:T(8,128)(2,1)} %bitcast.26, bf16[6,128,768]{2,1,0:T(8,128)(2,1)} %bitcast.25, bf16[6,128,768]{2,1,0:T(8,128)(2,1)} %bitcast.27), custom_call_target="tpu_custom_call" | custom-call | flops 2113929216 | bytes 2359296 | tf_op jit(solution)/shard_map/attend/pallas_call | solution.py:367
  141.6 47.5 %finish.1 = bf16[384,768]{1,0:T(8,128)(2,1)} custom-call(bf16[2,384,384]{2,1,0:T(8,128)(2,1)} %bitcast.16, bf16[768,3072]{1,0:T(8,128)(2,1)} %w_out.1, f32[1,768]{1,0:T(1,128)} %reshape.37.gate), custom_call_target="tpu_custom_call" | custom-call | tf_op jit(solution)/shard_map/finish/pallas_call | solution.py:486
  189.1 1.9 %copy.14 = bf16[384,768]{1,0:T(8,128)(2,1)} copy(bf16[384,768]{1,0:T(8,128)(2,1)} %finish.1) | data formatting | bytes 1179648
  (1 shorter events, 0.0 us)
Async XLA Ops:
  90.4 20.9 %copy-start.2 = (s32[3]{0:T(128)S(1)}, s32[3]{0:T(128)}, u32[]{:S(2)}) copy-start(s32[3]{0:T(128)} %param.19) | copy-start | bytes 40
  90.5 21.0 %copy-start.1 = (s32[3,14]{1,0:T(4,128)S(1)}, s32[3,14]{1,0:T(4,128)}, u32[]{:S(2)}) copy-start(s32[3,14]{1,0:T(4,128)} %param.18) | copy-start | bytes 508
  90.5 22.3 %copy-start = (f32[768]{0:T(1024)S(1)}, f32[768]{0:T(1024)}, u32[]{:S(2)}) copy-start(f32[768]{0:T(1024)} %param.15) | copy-start | bytes 9220
  107.7 15.9 %collective-permute-start.2 = (bf16[2,3,128,768]{3,2,1,0:T(8,128)(2,1)}, bf16[2,3,128,768]{3,2,1,0:T(8,128)(2,1)S(1)}, u32[]{:S(2)}, u32[]{:S(2)}) collective-permute-start(bf16[2,3,128,768]{3,2,1,0:T(8,128)(2,1)} %bitcast.23), channel_id=1, source_target_pairs={{0,4},{4,1},{1,5},{2,6},{6,3},{3,7},{8,12},{12,9},{9,13},{10,14},{... | collective-permute-start | bytes 3538952 | tf_op jit(solution)/shard_map/ppermute | solution.py:567
  110.1 13.6 %collective-permute-start.3 = (bf16[2,3,128,768]{3,2,1,0:T(8,128)(2,1)}, bf16[2,3,128,768]{3,2,1,0:T(8,128)(2,1)S(1)}, u32[]{:S(2)}, u32[]{:S(2)}) collective-permute-start(bf16[2,3,128,768]{3,2,1,0:T(8,128)(2,1)} %bitcast.24), channel_id=1, source_target_pairs={{4,0},{1,4},{5,1},{6,2},{3,6},{7,3},{12,8},{9,12},{13,9},{14,10},{... | collective-permute-start | bytes 3538952 | tf_op jit(solution)/shard_map/ppermute | solution.py:568
  111.6 10.7 %collective-permute-start.1 = (s32[3,15]{1,0:T(4,128)S(1)}, s32[3,15]{1,0:T(4,128)S(1)}, u32[]{:S(2)}, u32[]{:S(2)}) collective-permute-start(s32[3,15]{1,0:T(4,128)S(1)} %pad_add_fusion), channel_id=1, source_target_pairs={{16,0},{18,1},{20,2},{22,3},{17,4},{19,5},{21,6},{23,7},{24,8},{26... | collective-permute-start | bytes 548 | tf_op jit(solution)/shard_map/ppermute | solution.py:553
  112.1 10.2 %collective-permute-start = (s32[3,15]{1,0:T(4,128)S(1)}, s32[3,15]{1,0:T(4,128)S(1)}, u32[]{:S(2)}, u32[]{:S(2)}) collective-permute-start(s32[3,15]{1,0:T(4,128)S(1)} %pad_add_fusion), channel_id=1, source_target_pairs={{0,0},{2,1},{4,2},{6,3},{1,4},{3,5},{5,6},{7,7},{8,8},{10,9},{12,1... | collective-permute-start | bytes 548 | tf_op jit(solution)/shard_map/ppermute | solution.py:552
  123.7 1.0 copy-start.3
  123.7 1.4 copy-start.4

commit v4 on v3

--- a/solution.py
+++ b/solution.py
@@ -166,7 +166,8 @@
                 ))
         return copies, pltpu.make_async_copy(src, tok.at[e, t], local.at[q])
 
-    for q in range(2):
+    for n in range(2):
+        q = jnp.where(b < 2, n, 1 - n)
         source = 2 * (b % 2) + q
 
         def send(src, q=q):

time: 190 us -> 191 us (level); the launches traced: 191 us -> 189 us
    pallas_call x1, Pallas kernels: 47.5 us -> 44.6 us  [finish(): pl.pallas_call(functools.partial(finish_kernel, tps), out_shape=jax.Shape...]
where the time goes in v4:
time: 191 us; the launch traced here: 189 us
  Pallas kernels  176 us (92%)
  local copies, waits for them, and re-layouts  6.4 us (3%)
  starting transfers between devices  4.84 us (3%)
  other arithmetic  2.24 us (1%)
    pallas_call x1, Pallas kernels, gather_all(): pl.pallas_call(functools.partial(gather_kernel, tps, chunks), out_shape=(...  87.3 us
    pallas_call x1, Pallas kernels, finish(): pl.pallas_call(functools.partial(finish_kernel, tps), out_shape=jax.Shape...  44.6 us
    pallas_call x2, Pallas kernels, project(): pl.pallas_call(functools.partial(proj_kernel, normalize, gain.shape[0]),...  26.1 us
    pallas_call x1, Pallas kernels, attention(): pl.pallas_call(functools.partial(attend_kernel, head_size), grid_spec=plt...  17.6 us
  transfers between devices with their start and end apart: 4, of which 0 were waited for; matrix products, arithmetic and copies ran while one was open for 1% of the time, Pallas kernels for 5%

profile of v4, /device:TPU:0, one launch (start us, length us, event | category | flops | bytes accessed | tf_op | source)
XLA Modules:
  0.0 189.2 jit_solution(7633718718063951639)
XLA Ops:
  0.0 1.6 dynamic-slice_bitcast_fusion.2
  1.6 1.5 pad_maximum_fusion.w_in
  3.1 87.3 %gather_all.1 = (bf16[2,4,384,768]{3,2,1,0:T(8,128)(2,1)}, bf16[4,3,768,384]{3,2,1,0:T(8,128)(2,1)}) custom-call(bf16[384,768]{1,0:T(8,128)(2,1)} %tok_in.1, bf16[3,768,384]{2,1,0:T(8,128)(2,1)} %pad_maximum_fusion.w_in), custom_call_target="tpu_custom_call" | custom-call | tf_op jit(solution)/shard_map/gather_all/pallas_call | solution.py:275
  90.4 0.0 copy-start.2
  90.5 0.0 copy-start.1
  90.5 0.0 copy-start
  90.5 17.2 %project.3 = bf16[768,768]{1,0:T(8,128)(2,1)} custom-call(bf16[2,4,384,768]{3,2,1,0:T(8,128)(2,1)} %get-tuple-element.7.x_ref, f32[1,3072]{1,0:T(1,128)} %bitcast.17, f32[1,3072]{1,0:T(1,128)} %bitcast.19, bf16[4,3,768,384]{3,2,1,0:T(8,128)(2,1)} %get-tuple-element.8.w_ref, f32[1,128]{1,0:T(1,128)} %bitcast.28), custom_call_target="tpu_custom_call" | custom-call | flops 3623878656 | bytes 9437184 | tf_op jit(solution)/shard_map/project/pallas_call | solution.py:59
  107.7 2.3 %collective-permute-start.2 = (bf16[2,3,128,768]{3,2,1,0:T(8,128)(2,1)}, bf16[2,3,128,768]{3,2,1,0:T(8,128)(2,1)S(1)}, u32[]{:S(2)}, u32[]{:S(2)}) collective-permute-start(bf16[2,3,128,768]{3,2,1,0:T(8,128)(2,1)} %bitcast.23), channel_id=1, source_target_pairs={{0,4},{4,1},{1,5},{2,6},{6,3},{3,7},{8,12},{12,9},{9,13},{10,14},{... | collective-permute-start | bytes 3538952 | tf_op jit(solution)/shard_map/ppermute | solution.py:568
  110.1 1.3 collective-permute-start.3
  111.4 0.0 copy-done.2
  111.4 0.1 copy.12
  111.5 0.0 copy-done.1
  111.5 0.1 pad_add_fusion
  111.6 0.6 collective-permute-start.1
  112.1 0.6 collective-permute-start
  112.8 0.0 copy-done
  112.8 0.6 reshape.37.gate
  113.4 8.9 %project.2.q_ref = bf16[768,384]{1,0:T(8,128)(2,1)} custom-call(bf16[2,4,384,768]{3,2,1,0:T(8,128)(2,1)} %get-tuple-element.7.x_ref, f32[1,3072]{1,0:T(1,128)} %bitcast.18, f32[1,3072]{1,0:T(1,128)} %bitcast.20, bf16[4,3,768,384]{3,2,1,0:T(8,128)(2,1)} %get-tuple-element.8.w_ref, f32[1,128]{1,0:T(1,128)} %bitcast.21), custom_call_target="tpu_custom_call" | custom-call | flops 1811939328 | bytes 7077888 | tf_op jit(solution)/shard_map/project/pallas_call | solution.py:59
  122.3 0.0 collective-permute-done.1
  122.3 0.0 collective-permute-done
  122.3 0.8 slice_reduce_fusion.count_ref
  123.1 0.6 fusion.6.place_ref
  123.7 0.0 collective-permute-done.2
  123.7 0.0 copy-start.3
  123.7 0.0 collective-permute-done.3
  123.7 0.0 copy-start.4
  123.7 1.0 copy-done.3
  124.7 0.4 copy-done.4
  125.1 17.6 %attend.1 = bf16[768,384]{1,0:T(8,128)(2,1)} custom-call(s32[6,14]{1,0:T(8,128)} %fusion.6.place_ref, s32[6]{0:T(128)} %slice_reduce_fusion.count_ref, bf16[768,384]{1,0:T(8,128)(2,1)} %project.2.q_ref, bf16[6,128,768]{2,1,0:T(8,128)(2,1)} %bitcast.26, bf16[6,128,768]{2,1,0:T(8,128)(2,1)} %bitcast.25, bf16[6,128,768]{2,1,0:T(8,128)(2,1)} %bitcast.27), custom_call_target="tpu_custom_call" | custom-call | flops 2113929216 | bytes 2359296 | tf_op jit(solution)/shard_map/attend/pallas_call | solution.py:368
  142.7 44.6 %finish.1 = bf16[384,768]{1,0:T(8,128)(2,1)} custom-call(bf16[2,384,384]{2,1,0:T(8,128)(2,1)} %bitcast.16, bf16[768,3072]{1,0:T(8,128)(2,1)} %w_out.1, f32[1,768]{1,0:T(1,128)} %reshape.37.gate), custom_call_target="tpu_custom_call" | custom-call | tf_op jit(solution)/shard_map/finish/pallas_call | solution.py:487
  187.3 1.9 %copy.14 = bf16[384,768]{1,0:T(8,128)(2,1)} copy(bf16[384,768]{1,0:T(8,128)(2,1)} %finish.1) | data formatting | bytes 1179648
  (1 shorter events, 0.0 us)
Async XLA Ops:
  90.4 20.9 %copy-start.2 = (s32[3]{0:T(128)S(1)}, s32[3]{0:T(128)}, u32[]{:S(2)}) copy-start(s32[3]{0:T(128)} %param.19) | copy-start | bytes 40
  90.5 21.0 %copy-start.1 = (s32[3,14]{1,0:T(4,128)S(1)}, s32[3,14]{1,0:T(4,128)}, u32[]{:S(2)}) copy-start(s32[3,14]{1,0:T(4,128)} %param.18) | copy-start | bytes 508
  90.5 22.3 %copy-start = (f32[768]{0:T(1024)S(1)}, f32[768]{0:T(1024)}, u32[]{:S(2)}) copy-start(f32[768]{0:T(1024)} %param.15) | copy-start | bytes 9220
  107.7 15.9 %collective-permute-start.2 = (bf16[2,3,128,768]{3,2,1,0:T(8,128)(2,1)}, bf16[2,3,128,768]{3,2,1,0:T(8,128)(2,1)S(1)}, u32[]{:S(2)}, u32[]{:S(2)}) collective-permute-start(bf16[2,3,128,768]{3,2,1,0:T(8,128)(2,1)} %bitcast.23), channel_id=1, source_target_pairs={{0,4},{4,1},{1,5},{2,6},{6,3},{3,7},{8,12},{12,9},{9,13},{10,14},{... | collective-permute-start | bytes 3538952 | tf_op jit(solution)/shard_map/ppermute | solution.py:568
  110.1 13.6 %collective-permute-start.3 = (bf16[2,3,128,768]{3,2,1,0:T(8,128)(2,1)}, bf16[2,3,128,768]{3,2,1,0:T(8,128)(2,1)S(1)}, u32[]{:S(2)}, u32[]{:S(2)}) collective-permute-start(bf16[2,3,128,768]{3,2,1,0:T(8,128)(2,1)} %bitcast.24), channel_id=1, source_target_pairs={{4,0},{1,4},{5,1},{6,2},{3,6},{7,3},{12,8},{9,12},{13,9},{14,10},{... | collective-permute-start | bytes 3538952 | tf_op jit(solution)/shard_map/ppermute | solution.py:569
  111.6 10.7 %collective-permute-start.1 = (s32[3,15]{1,0:T(4,128)S(1)}, s32[3,15]{1,0:T(4,128)S(1)}, u32[]{:S(2)}, u32[]{:S(2)}) collective-permute-start(s32[3,15]{1,0:T(4,128)S(1)} %pad_add_fusion), channel_id=1, source_target_pairs={{16,0},{18,1},{20,2},{22,3},{17,4},{19,5},{21,6},{23,7},{24,8},{26... | collective-permute-start | bytes 548 | tf_op jit(solution)/shard_map/ppermute | solution.py:554
  112.1 10.2 %collective-permute-start = (s32[3,15]{1,0:T(4,128)S(1)}, s32[3,15]{1,0:T(4,128)S(1)}, u32[]{:S(2)}, u32[]{:S(2)}) collective-permute-start(s32[3,15]{1,0:T(4,128)S(1)} %pad_add_fusion), channel_id=1, source_target_pairs={{0,0},{2,1},{4,2},{6,3},{1,4},{3,5},{5,6},{7,7},{8,8},{10,9},{12,1... | collective-permute-start | bytes 548 | tf_op jit(solution)/shard_map/ppermute | solution.py:553
  123.7 1.0 copy-start.3
  123.7 1.4 copy-start.4
